TPU v7x, 128 devices: a whole 4x4x4 slice. The times are simulated.
128 devices in a mesh: lat: 8 (over y, core), lon: 16 (over x, z).
Axes of the slice: x: 4, y: 4, z: 4, core: 2. Of those that a mesh axis runs over, the one named last changes fastest.
Arguments:
- state: float32 [4, 80, 64, 2048], P(None, None, 'lat', 'lon'), may hold values from -4 to 4
- mixing: float32 [64, 2048], P('lat', 'lon'), may hold values from 0.2 to 5
- insolation: float32 [64, 2048], P('lat', 'lon'), may hold values from 0 to 1
- filter_rows: int32 [64], replicated, may hold values 0 or 1
- block_map: int32 [64, 2048], P('lat', 'lon'), may hold values from 0 to 131071, as said below
Outputs:
- state_out: float32 [4, 80, 64, 2048], P(None, None, 'lat', 'lon')
- block_heating: float32 [128, 80, 1024], P(('lat', 'lon'))
Inputs may be any that keep to these rules, and one draw needn't show every extreme that they name: `block_map`: blocks are numbered like the devices of the lat+lon axes. The 1024 columns of every device's tile give exactly 8 columns to each block, and each block's 1024 slots are each named by exactly one column.
All inputs are finite; a program needn't handle non-finite values.
Results may differ from a plain program's by a relative error of at most 0.0001.
Values sent between devices are 32-bit elements; how exact they have to be, the bound alone decides.
No kernel may reach another device: no remote copies, remote signals or barrier semaphores. Data moves between devices by JAX's collectives and lax.ppermute only.
A program may use at most 64 MiB of HBM per device.

v0:
```python
import math

import jax
import jax.numpy as jnp
import numpy as np
from jax import lax
from jax.experimental import pallas as pl
from jax.experimental.pallas import tpu as pltpu
from jax.sharding import PartitionSpec as P

KEEP = 64
ADVECT = 0.1
DIFFUSE = 0.1
ROTATE = 0.2
RADIATE = 0.5
FLOOR = 0.25

FIELDS = 4
LEVELS = 80
ROWS = 8
COLS = 128
N_LAT = 8
N_LON = 16
GROUP = LEVELS // N_LON
PAIRS = FIELDS * GROUP
MAIN = PAIRS * ROWS
EDGE = 2 * PAIRS
EDGE_PAD = 48
ALL = MAIN + EDGE_PAD
COLUMNS = ROWS * COLS
BLOCKS = N_LAT * N_LON
CIRCLE = COLS * N_LON

F32 = jnp.float32
BF16 = jnp.bfloat16
VMEM = pl.BlockSpec(memory_space=pltpu.VMEM)
SMEM = pl.BlockSpec(memory_space=pltpu.SMEM)


def halves(values):
    high = values.astype(BF16)
    low = (values - high.astype(F32)).astype(BF16)
    return high, low


def fourier_tables():
    waves = np.arange(KEEP)
    phase = 2.0 * math.pi / CIRCLE * (np.outer(np.arange(CIRCLE), waves) % CIRCLE)
    analysis = np.concatenate([np.cos(phase), np.sin(phase)], axis=1)
    weights = np.where(waves == 0, 1.0, 2.0)[:, None] / CIRCLE
    synthesis = np.concatenate([weights * np.cos(phase.T), weights * np.sin(phase.T)], axis=0)

    def split(table, axis):
        high = table.astype(BF16)
        low = (table - high.astype(np.float64)).astype(BF16)
        return np.concatenate([high, low], axis=axis)

    return split(analysis, 1), split(synthesis, 0)


def row_tables():
    total = N_LAT * ROWS
    table = np.zeros((N_LAT, 8, ROWS, COLS), np.float32)
    rows = np.arange(-1, total + 1)
    latitude = (rows + 0.5) * (math.pi / total) - 0.5 * math.pi
    metric = 1.0 / np.maximum(np.cos(latitude), FLOOR)
    coriolis = np.sin(latitude)
    for band in range(N_LAT):
        first = band * ROWS
        table[band, 0] = metric[first + 1 : first + 1 + ROWS, None]
        table[band, 1] = coriolis[first + 1 : first + 1 + ROWS, None]
        table[band, 2] = metric[first + 1 + ROWS]
        table[band, 3] = coriolis[first + 1 + ROWS]
        table[band, 4] = float(band < N_LAT - 1)
        table[band, 5] = metric[first]
        table[band, 6] = coriolis[first]
        table[band, 7] = float(band > 0)
    return table


def pack_kernel(state_ref, low_ref, high_ref):
    for tile in range(N_LON):
        for place, row in enumerate((0, 1)):
            low_ref[tile, pl.ds(place * PAIRS, PAIRS), :] = state_ref[
                tile, pl.ds(row, PAIRS, stride=ROWS), :
            ]
        for place, row in enumerate((ROWS - 2, ROWS - 1)):
            high_ref[tile, pl.ds(place * PAIRS, PAIRS), :] = state_ref[
                tile, pl.ds(row, PAIRS, stride=ROWS), :
            ]


def stencil(center, east, west, north, south, zonal, meridional, metric):
    stepped = center - ADVECT * (
        zonal * metric * (east - west) + meridional * (north - south)
    )
    return stepped + DIFFUSE * (east + west + north + south - 4.0 * center)


def turned(field, zonal, meridional, coriolis):
    if field == 0:
        return ROTATE * coriolis * meridional
    if field == 1:
        return -ROTATE * coriolis * zonal
    return None


def dynamics_kernel(
    band_ref, filter_ref, state_ref, north_ref, south_ref, rows_ref, analysis_ref, synthesis_ref,
    out_ref, stepped_ref, current_ref, split_ref,
):
    band = band_ref[0]
    first = band * ROWS
    lane = lax.broadcasted_iota(jnp.int32, (ROWS, COLS), 1)
    sub = lax.broadcasted_iota(jnp.int32, (ROWS, COLS), 0)
    lane_edge = lane[:GROUP]
    metric = rows_ref[band, 0]
    coriolis = rows_ref[band, 1]

    def beside(load, tile, lanes):
        here = load(tile)
        after = load((tile + 1) % N_LON)
        before = load((tile - 1) % N_LON)
        east = jnp.where(
            lanes == COLS - 1, pltpu.roll(after, COLS - 1, 1), pltpu.roll(here, COLS - 1, 1)
        )
        west = jnp.where(lanes == 0, pltpu.roll(before, 1, 1), pltpu.roll(here, 1, 1))
        return here, east, west

    def step_main(source, north_of, south_of):
        def level_step(level, carry):
            for field in range(FIELDS):
                at = pl.ds(pl.multiple_of((field * GROUP + level) * ROWS, ROWS), ROWS)
                at_u = pl.ds(pl.multiple_of(level * ROWS, ROWS), ROWS)
                at_v = pl.ds(pl.multiple_of((GROUP + level) * ROWS, ROWS), ROWS)
                pair = field * GROUP + level
                for tile in range(N_LON):
                    here, east, west = beside(lambda t: source[t, at, :], tile, lane)
                    north = jnp.where(
                        sub == ROWS - 1, north_of(tile, pair), pltpu.roll(here, ROWS - 1, 0)
                    )
                    south = jnp.where(sub == 0, south_of(tile, pair), pltpu.roll(here, 1, 0))
                    zonal = source[tile, at_u, :]
                    meridional = source[tile, at_v, :]
                    result = stencil(here, east, west, north, south, zonal, meridional, metric)
                    extra = turned(field, zonal, meridional, coriolis)
                    if extra is not None:
                        result = result + extra
                    stepped_ref[tile, at, :] = result
            return carry

        lax.fori_loop(0, GROUP, level_step, 0)

    def step_edge(side):
        base = 2 + 3 * side
        metric_edge = rows_ref[band, base][:GROUP]
        coriolis_edge = rows_ref[band, base + 1][:GROUP]
        exists = rows_ref[band, base + 2][:GROUP]
        halo = (north_ref, south_ref)[side]
        near = (0, PAIRS)[side]
        far = (PAIRS, 0)[side]
        for tile in range(N_LON):
            zonal = halo[tile, near : near + GROUP, :]
            meridional = halo[tile, near + GROUP : near + 2 * GROUP, :]
            for field in range(FIELDS):
                at = near + field * GROUP
                here, east, west = beside(lambda t: halo[t, at : at + GROUP, :], tile, lane_edge)
                outer = halo[tile, far + field * GROUP : far + (field + 1) * GROUP, :]
                inner = state_ref[
                    tile,
                    pl.ds(field * GROUP * ROWS + (ROWS - 1, 0)[side], GROUP, stride=ROWS),
                    :,
                ]
                north, south = ((outer, inner), (inner, outer))[side]
                result = stencil(
                    here, east, west, north, south, zonal, meridional, metric_edge
                )
                extra = turned(field, zonal, meridional, coriolis_edge)
                if extra is not None:
                    result = result + extra
                place = MAIN + side * PAIRS + field * GROUP
                stepped_ref[tile, place : place + GROUP, :] = jnp.where(exists > 0.5, result, 0.0)

    wanted = jnp.zeros((ROWS, COLS), jnp.int32)
    for row in range(ROWS):
        wanted = jnp.where(sub == row, filter_ref[first + row], wanted)
    wanted_main = jnp.concatenate([wanted] * PAIRS, axis=0) == 1
    wanted_above = filter_ref[jnp.minimum(first + ROWS, N_LAT * ROWS - 1)]
    wanted_below = filter_ref[jnp.maximum(first - 1, 0)]
    edge_row = lax.broadcasted_iota(jnp.int32, (EDGE_PAD, COLS), 0)
    wanted_edge = jnp.where(edge_row < PAIRS, wanted_above, wanted_below) == 1

    def polar_filter(rows, target):
        for tile in range(N_LON):
            high, low = halves(stepped_ref[tile, :rows, :])
            split_ref[:rows, tile * COLS : (tile + 1) * COLS] = high
            split_ref[rows : 2 * rows, tile * COLS : (tile + 1) * COLS] = low
        sums = jnp.dot(split_ref[: 2 * rows, :], analysis_ref[...], preferred_element_type=F32)
        sums = sums[:rows] + sums[rows:]
        sums = sums[:, :COLS] + sums[:, COLS:]
        high, low = halves(sums)
        both = jnp.concatenate(
            [jnp.concatenate([high, high], axis=1), jnp.concatenate([low, low], axis=1)], axis=0
        )
        for pair in range(N_LON // 2):
            smooth = jnp.dot(
                both,
                synthesis_ref[:, pair * 2 * COLS : (pair + 1) * 2 * COLS],
                preferred_element_type=F32,
            )
            smooth = smooth[:rows] + smooth[rows:]
            for side in range(2):
                tile = 2 * pair + side
                piece = smooth[:, side * COLS : (side + 1) * COLS]
                target[tile, :MAIN, :] = jnp.where(
                    wanted_main, piece[:MAIN], stepped_ref[tile, :MAIN, :]
                )
                if rows > MAIN:
                    target[tile, MAIN:rows, :] = jnp.where(
                        wanted_edge, piece[MAIN:], stepped_ref[tile, MAIN:rows, :]
                    )

    stepped_ref[:, MAIN + EDGE :, :] = jnp.zeros((N_LON, ALL - MAIN - EDGE, COLS), F32)
    step_main(
        state_ref,
        lambda tile, pair: north_ref[tile, pl.ds(pair, 1), :],
        lambda tile, pair: south_ref[tile, pl.ds(PAIRS + pair, 1), :],
    )
    step_edge(0)
    step_edge(1)
    polar_filter(ALL, current_ref)
    step_main(
        current_ref,
        lambda tile, pair: current_ref[tile, pl.ds(MAIN + pair, 1), :],
        lambda tile, pair: current_ref[tile, pl.ds(MAIN + PAIRS + pair, 1), :],
    )
    polar_filter(MAIN, out_ref)


def prepare_kernel(mixing_ref, map_ref, gain_ref, inverse_ref, order_ref):
    mix = mixing_ref[...]

    def level_step(level, above):
        inside = jnp.where((level == 0) | (level == LEVELS - 1), 1.0, 2.0)
        inverse = 1.0 / (1.0 + inside * mix - mix * above)
        gain = mix * inverse
        gain_ref[level] = gain
        inverse_ref[level] = inverse
        return gain

    lax.fori_loop(0, LEVELS, level_step, jnp.zeros_like(mix))

    target = map_ref[...] // COLUMNS
    before = lax.broadcasted_iota(jnp.int32, (COLS, 2 * COLS), 0)
    after = lax.broadcasted_iota(jnp.int32, (COLS, 2 * COLS), 1)
    counter = jnp.where((before < after) | (after >= COLS), 1.0, 0.0).astype(BF16)
    block = lax.broadcasted_iota(jnp.int32, (BLOCKS, COLS), 0)
    place = lax.broadcasted_iota(jnp.int32, (COLUMNS, COLS), 0)
    earlier = jnp.zeros((BLOCKS, COLS), F32)
    for row in range(ROWS):
        goal = target[row : row + 1, :]
        chosen = jnp.where(block == goal, 1.0, 0.0)
        counted = jnp.dot(chosen.astype(BF16), counter, preferred_element_type=F32)
        rank = jnp.sum(chosen * (counted[:, :COLS] + earlier), axis=0, keepdims=True)
        earlier = earlier + counted[:, COLS:]
        seat = goal * ROWS + rank.astype(jnp.int32)
        order_ref[:, row * COLS : (row + 1) * COLS] = jnp.where(place == seat, 1.0, 0.0).astype(BF16)


def physics_kernel(
    dyn_ref, mixing_ref, sun_ref, map_ref, gain_ref, inverse_ref, order_ref,
    out_ref, send_ref, heating_ref, table_ref,
):
    zero = jnp.zeros((ROWS, COLS), F32)

    def forward(group, carry):
        for inner in range(GROUP):
            level = group * GROUP + inner
            gain = gain_ref[level]
            inverse = inverse_ref[level]
            carry = tuple(
                dyn_ref[group, (field * GROUP + inner) * ROWS : (field * GROUP + inner + 1) * ROWS, :]
                * inverse
                + gain * carry[field]
                for field in range(FIELDS)
            )
            for field in range(FIELDS):
                out_ref[field, level] = carry[field]
        return carry

    lax.fori_loop(0, N_LON, forward, (zero,) * FIELDS)
    sun = RADIATE * sun_ref[...]

    def backward(step, carry):
        group = N_LON - 1 - step
        for inner in reversed(range(GROUP)):
            level = group * GROUP + inner
            gain = gain_ref[level]
            carry = tuple(out_ref[field, level] + gain * carry[field] for field in range(FIELDS))
            warmed = carry[2] + sun * carry[3]
            out_ref[0, level] = carry[0]
            out_ref[1, level] = carry[1]
            out_ref[2, level] = warmed
            out_ref[3, level] = carry[3]
            at = (2 * GROUP + inner) * ROWS
            heating_ref[pl.ds(pl.multiple_of(level * ROWS, ROWS), ROWS), :] = (
                warmed - dyn_ref[group, at : at + ROWS, :]
            )
        return carry

    lax.fori_loop(0, N_LON, backward, (zero,) * FIELDS)

    slots = (map_ref[...] % COLUMNS).astype(F32)
    top = lax.broadcasted_iota(jnp.int32, (COLS - LEVELS, COLS), 0) == 0
    for row in range(ROWS):
        body = heating_ref[pl.ds(row, LEVELS, stride=ROWS), :]
        tail = jnp.where(top, slots[row : row + 1, :], 0.0)
        high, low = halves(jnp.concatenate([body, tail], axis=0))
        table_ref[:COLS, row * COLS : (row + 1) * COLS] = high
        table_ref[COLS:, row * COLS : (row + 1) * COLS] = low
    sent = lax.dot_general(
        order_ref[...], table_ref[...], (((1,), (1,)), ((), ())), preferred_element_type=F32
    )
    send_ref[...] = sent[:, :COLS] + sent[:, COLS:]


def place_kernel(got_ref, out_ref):
    got = got_ref[...]
    slot = got[:, LEVELS : LEVELS + 1]
    column = lax.broadcasted_iota(jnp.int32, (COLUMNS, COLUMNS), 1).astype(F32)
    chosen = jnp.where(column == slot, 1.0, 0.0).astype(BF16)
    high, low = halves(got.T[:LEVELS])
    both = jnp.concatenate([high, low], axis=0)
    placed = jnp.dot(both, chosen, preferred_element_type=F32)
    out_ref[0] = placed[:LEVELS] + placed[LEVELS:]


def per_device(state, mixing, insolation, filter_rows, block_map):
    analysis, synthesis = (jnp.asarray(table) for table in fourier_tables())
    rows = jnp.asarray(row_tables())
    band = lax.axis_index("lat").astype(jnp.int32).reshape(1)
    up = [(i, i + 1) for i in range(N_LAT - 1)]
    down = [(i + 1, i) for i in range(N_LAT - 1)]

    by_group = state.reshape(FIELDS, N_LON, GROUP, ROWS, COLS).transpose(1, 0, 2, 3, 4)
    circles = lax.all_to_all(
        by_group.reshape(N_LON, MAIN, COLS), "lon", split_axis=0, concat_axis=0, tiled=True
    )
    edge = jax.ShapeDtypeStruct((N_LON, EDGE, COLS), F32)
    first_rows, last_rows = pl.pallas_call(
        pack_kernel, out_shape=(edge, edge), in_specs=[VMEM], out_specs=(VMEM, VMEM), name="pack"
    )(circles)
    north = lax.ppermute(first_rows, "lat", down)
    south = lax.ppermute(last_rows, "lat", up)
    dyn = pl.pallas_call(
        dynamics_kernel,
        out_shape=jax.ShapeDtypeStruct((N_LON, MAIN, COLS), F32),
        in_specs=[SMEM, SMEM] + [VMEM] * 6,
        out_specs=VMEM,
        scratch_shapes=[
            pltpu.VMEM((N_LON, ALL, COLS), F32),
            pltpu.VMEM((N_LON, ALL, COLS), F32),
            pltpu.VMEM((2 * ALL, CIRCLE), BF16),
        ],
        name="dynamics",
    )(band, filter_rows, circles, north, south, rows, analysis, synthesis)
    levels = jax.ShapeDtypeStruct((LEVELS, ROWS, COLS), F32)
    gain, inverse, order = pl.pallas_call(
        prepare_kernel,
        out_shape=(levels, levels, jax.ShapeDtypeStruct((COLUMNS, COLUMNS), BF16)),
        in_specs=[VMEM] * 2,
        out_specs=(VMEM,) * 3,
        name="prepare",
    )(mixing, block_map)
    columns = lax.all_to_all(dyn, "lon", split_axis=0, concat_axis=0, tiled=True)
    new_state, sent = pl.pallas_call(
        physics_kernel,
        out_shape=(
            jax.ShapeDtypeStruct((FIELDS, LEVELS, ROWS, COLS), F32),
            jax.ShapeDtypeStruct((COLUMNS, COLS), F32),
        ),
        in_specs=[VMEM] * 7,
        out_specs=(VMEM,) * 2,
        scratch_shapes=[
            pltpu.VMEM((LEVELS * ROWS, COLS), F32),
            pltpu.VMEM((2 * COLS, COLUMNS), BF16),
        ],
        name="physics",
    )(columns, mixing, insolation, block_map, gain, inverse, order)
    got = lax.all_to_all(
        sent.reshape(BLOCKS, ROWS, COLS), ("lat", "lon"), split_axis=0, concat_axis=0, tiled=True
    )
    block_heating = pl.pallas_call(
        place_kernel,
        out_shape=jax.ShapeDtypeStruct((1, LEVELS, COLUMNS), F32),
        in_specs=[VMEM],
        out_specs=VMEM,
        name="place",
    )(got.reshape(COLUMNS, COLS))
    return new_state, block_heating


def solution(mesh):
    in_specs = (P(None, None, "lat", "lon"), P("lat", "lon"), P("lat", "lon"), P(), P("lat", "lon"))
    out_specs = (P(None, None, "lat", "lon"), P(("lat", "lon"), None, None))
    return jax.shard_map(
        per_device, mesh=mesh, in_specs=in_specs, out_specs=out_specs, check_vma=False
    )
```

profile of v0, /device:TPU:1, one launch (start us, length us, event | category | flops | bytes accessed | tf_op | source)
XLA Modules:
  0.0 105.6 jit_solution(6386402765800709526)
XLA Ops:
  0.6 1.4 %copy.10 = f32[4,16,5,8,128]{4,3,2,0,1:T(8,128)S(1)} copy(f32[4,16,5,8,128]{4,3,2,1,0:T(8,128)} %bitcast.9) | data formatting | bytes 2621440 | tf_op jit(solution)/shard_map/reshape | solution.py:345
  2.1 27.3 %all_to_all.15.state_ref = f32[16,160,128]{2,1,0:T(8,128)} all-to-all(f32[16,160,128]{2,1,0:T(8,128)S(1)} %bitcast.7), channel_id=1, replica_groups=mesh['lat'=8,'lon'=16] {'lon'}, dimensions={0} | all-to-all | bytes 2621440 | tf_op jit(solution)/shard_map/all_to_all | solution.py:346
  29.4 2.3 %pack.1 = (f32[16,40,128]{2,1,0:T(8,128)}, f32[16,40,128]{2,1,0:T(8,128)}) custom-call(f32[16,160,128]{2,1,0:T(8,128)} %all_to_all.15.state_ref), custom_call_target="tpu_custom_call" | custom-call | tf_op jit(solution)/shard_map/pack/pallas_call | solution.py:350
  31.6 3.6 %collective-permute-start = (f32[16,40,128]{2,1,0:T(8,128)}, f32[16,40,128]{2,1,0:T(8,128)S(1)}, u32[]{:S(2)}, u32[]{:S(2)}) collective-permute-start(f32[16,40,128]{2,1,0:T(8,128)} %get-tuple-element.9), channel_id=1, source_target_pairs={{16,0},{32,16},{48,32},{64,48},{80,64},{96,80},{112,96},{17,1},{33... | collective-permute-start | bytes 983048 | tf_op jit(solution)/shard_map/ppermute | solution.py:353
  35.3 3.1 %collective-permute-start.1 = (f32[16,40,128]{2,1,0:T(8,128)}, f32[16,40,128]{2,1,0:T(8,128)S(1)}, u32[]{:S(2)}, u32[]{:S(2)}) collective-permute-start(f32[16,40,128]{2,1,0:T(8,128)} %get-tuple-element.10), channel_id=1, source_target_pairs={{0,16},{16,32},{32,48},{48,64},{64,80},{80,96},{96,112},{1,17},{17... | collective-permute-start | bytes 983048 | tf_op jit(solution)/shard_map/ppermute | solution.py:354
  38.4 3.0 %collective-permute-done.north_ref = f32[16,40,128]{2,1,0:T(8,128)S(1)} collective-permute-done((f32[16,40,128]{2,1,0:T(8,128)}, f32[16,40,128]{2,1,0:T(8,128)S(1)}, u32[]{:S(2)}, u32[]{:S(2)}) %collective-permute-start) | collective-permute-done | bytes 327712 | tf_op jit(solution)/shard_map/ppermute | solution.py:353
  41.4 0.0 copy-start.1
  41.4 1.3 %collective-permute-done.1.south_ref = f32[16,40,128]{2,1,0:T(8,128)S(1)} collective-permute-done((f32[16,40,128]{2,1,0:T(8,128)}, f32[16,40,128]{2,1,0:T(8,128)S(1)}, u32[]{:S(2)}, u32[]{:S(2)}) %collective-permute-start.1) | collective-permute-done | bytes 327712 | tf_op jit(solution)/shard_map/ppermute | solution.py:354
  42.7 0.0 copy-start.2
  42.7 0.0 copy-done.1
  42.7 0.7 copy-done.2
  43.4 10.4 %dynamics.1 = f32[16,160,128]{2,1,0:T(8,128)} custom-call(s32[1]{0:T(128)} %bitcast.band_ref, s32[64]{0:T(128)} %filter_ref.1, f32[16,160,128]{2,1,0:T(8,128)} %all_to_all.15.state_ref, f32[16,40,128]{2,1,0:T(8,128)} %copy-done.1, f32[16,40,128]{2,1,0:T(8,128)} %copy-done.2, f32[8,8,8,128]{3,2,1,0:T(8,128)} %constant.14.clone.rows_ref, ...), custom_call_target="tpu_custom_call" | custom-call | tf_op jit(solution)/shard_map/dynamics/pallas_call | solution.py:355
  53.9 3.7 %all-to-all-start.1 = ((f32[16,160,128]{2,1,0:T(8,128)}), f32[16,160,128]{2,1,0:T(8,128)S(1)}, u32[]{:S(2)}, u32[]{:S(2)}) async-start(f32[16,160,128]{2,1,0:T(8,128)} %dynamics.1), calls=%async_computation.1 | async-start | bytes 2621440 | tf_op jit(solution)/shard_map/all_to_all | solution.py:375
  57.6 4.6 %prepare.1 = (f32[80,8,128]{2,1,0:T(8,128)}, f32[80,8,128]{2,1,0:T(8,128)}, bf16[1024,1024]{1,0:T(8,128)(2,1)}) custom-call(f32[8,128]{1,0:T(8,128)} %mixing_ref.3, s32[8,128]{1,0:T(8,128)} %map_ref.3), custom_call_target="tpu_custom_call" | custom-call | tf_op jit(solution)/shard_map/prepare/pallas_call | solution.py:368
  62.1 12.9 %all-to-all-done.1.dyn_ref = f32[16,160,128]{2,1,0:T(8,128)S(1)} async-done(((f32[16,160,128]{2,1,0:T(8,128)}), f32[16,160,128]{2,1,0:T(8,128)S(1)}, u32[]{:S(2)}, u32[]{:S(2)}) %all-to-all-start.1) | async-done | bytes 1310752 | tf_op jit(solution)/shard_map/all_to_all | solution.py:375
  75.0 0.0 copy-start
  75.0 1.1 %copy-done = f32[16,160,128]{2,1,0:T(8,128)} copy-done((f32[16,160,128]{2,1,0:T(8,128)}, f32[16,160,128]{2,1,0:T(8,128)S(1)}, u32[]{:S(2)}) %copy-start) | copy-done | bytes 1310744
  76.1 4.4 %physics.1 = (f32[4,80,8,128]{3,2,1,0:T(8,128)}, f32[1024,128]{1,0:T(8,128)}) custom-call(f32[16,160,128]{2,1,0:T(8,128)} %copy-done, f32[8,128]{1,0:T(8,128)} %mixing_ref.3, f32[8,128]{1,0:T(8,128)} %sun_ref.1, s32[8,128]{1,0:T(8,128)} %map_ref.3, f32[80,8,128]{2,1,0:T(8,128)} %get-tuple-element.11.gain_ref, f32[80,8,128]{2,1,0:T(8,128)} %get-tuple-element.12.inverse_ref, ...), custom_call_target="tpu_custom_call" | custom-call | tf_op jit(solution)/shard_map/physics/pallas_call | solution.py:376
  80.5 22.6 %all_to_all.16 = f32[128,8,128]{2,1,0:T(8,128)} all-to-all(f32[128,8,128]{2,1,0:T(8,128)} %bitcast.10), channel_id=1, replica_groups=mesh['lat'=8,'lon'=16] {'lat','lon'}, dimensions={0} | all-to-all | bytes 1048576 | tf_op jit(solution)/shard_map/all_to_all | solution.py:390
  103.1 2.5 %place.1 = f32[1,80,1024]{2,1,0:T(8,128)} custom-call(f32[1024,128]{1,0:T(8,128)} %bitcast.8), custom_call_target="tpu_custom_call" | custom-call | tf_op jit(solution)/shard_map/place/pallas_call | solution.py:393
Async XLA Ops:
  31.6 9.8 %collective-permute-start = (f32[16,40,128]{2,1,0:T(8,128)}, f32[16,40,128]{2,1,0:T(8,128)S(1)}, u32[]{:S(2)}, u32[]{:S(2)}) collective-permute-start(f32[16,40,128]{2,1,0:T(8,128)} %get-tuple-element.9), channel_id=1, source_target_pairs={{16,0},{32,16},{48,32},{64,48},{80,64},{96,80},{112,96},{17,1},{33... | collective-permute-start | bytes 983048 | tf_op jit(solution)/shard_map/ppermute | solution.py:353
  35.3 7.4 %collective-permute-start.1 = (f32[16,40,128]{2,1,0:T(8,128)}, f32[16,40,128]{2,1,0:T(8,128)S(1)}, u32[]{:S(2)}, u32[]{:S(2)}) collective-permute-start(f32[16,40,128]{2,1,0:T(8,128)} %get-tuple-element.10), channel_id=1, source_target_pairs={{0,16},{16,32},{32,48},{48,64},{64,80},{80,96},{96,112},{1,17},{17... | collective-permute-start | bytes 983048 | tf_op jit(solution)/shard_map/ppermute | solution.py:354
  41.4 1.3 %copy-start.1 = (f32[16,40,128]{2,1,0:T(8,128)}, f32[16,40,128]{2,1,0:T(8,128)S(1)}, u32[]{:S(2)}) copy-start(f32[16,40,128]{2,1,0:T(8,128)S(1)} %collective-permute-done.north_ref) | copy-start | bytes 983044
  42.7 0.7 copy-start.2
  53.9 21.1 %all-to-all-start.1 = ((f32[16,160,128]{2,1,0:T(8,128)}), f32[16,160,128]{2,1,0:T(8,128)S(1)}, u32[]{:S(2)}, u32[]{:S(2)}) async-start(f32[16,160,128]{2,1,0:T(8,128)} %dynamics.1), calls=%async_computation.1 | async-start | bytes 2621440 | tf_op jit(solution)/shard_map/all_to_all | solution.py:375
  75.0 1.1 %copy-start = (f32[16,160,128]{2,1,0:T(8,128)}, f32[16,160,128]{2,1,0:T(8,128)S(1)}, u32[]{:S(2)}) copy-start(f32[16,160,128]{2,1,0:T(8,128)S(1)} %all-to-all-done.1.dyn_ref) | copy-start | bytes 3932164
where the time goes:
time: 106 us
  blocking collectives  49.9 us (47%)
  Pallas kernels  24.1 us (23%)
  waiting for transfers between devices  17.2 us (16%)
  starting transfers between devices  10.4 us (10%)
  local copies, waits for them, and re-layouts  3.24 us (3%)
    all_to_all x1, blocking collectives, per_device(): lax.all_to_all(by_group.reshape(N_LON, MAIN, COLS), 'lon', split_axis=0,...  27.3 us
    all_to_all x1, blocking collectives, per_device(): lax.all_to_all(sent.reshape(BLOCKS, ROWS, COLS), ('lat', 'lon'), split_ax...  22.6 us
    all_to_all x1, waiting for transfers between devices, per_device(): lax.all_to_all(dyn, 'lon', split_axis=0, concat_axis=0, tiled=True)  12.9 us
    pallas_call x1, Pallas kernels, per_device(): pl.pallas_call(dynamics_kernel, out_shape=jax.ShapeDtypeStruct((N_LON, MA...  10.4 us
    pallas_call x1, Pallas kernels, per_device(): pl.pallas_call(prepare_kernel, out_shape=(levels, levels, jax.ShapeDtypeS...  4.55 us
    pallas_call x1, Pallas kernels, per_device(): pl.pallas_call(physics_kernel, out_shape=(jax.ShapeDtypeStruct((FIELDS, L...  4.39 us
    all_to_all x1, starting transfers between devices, per_device(): lax.all_to_all(dyn, 'lon', split_axis=0, concat_axis=0, tiled=True)  3.7 us
    ppermute x1, starting transfers between devices, per_device(): north = lax.ppermute(first_rows, 'lat', down)  3.63 us
  transfers between devices with their start and end apart: 3, of which 3 were waited for; matrix products, arithmetic and copies ran while one was open for 0% of the time, Pallas kernels for 4%

commit v1 on v0

--- a/solution.py
+++ b/solution.py
@@ -34,7 +34,29 @@
 F32 = jnp.float32
 BF16 = jnp.bfloat16
 VMEM = pl.BlockSpec(memory_space=pltpu.VMEM)
+ANY = pl.BlockSpec(memory_space=pl.ANY)
 SMEM = pl.BlockSpec(memory_space=pltpu.SMEM)
+
+
+def call(kernel, name, out_shapes, scratch, megabytes, *args, scalars=0, stored=(), after=()):
+    def body(*refs):
+        kernel(*refs[: len(args)], *refs[len(args) + len(after) :])
+
+    placed = args[:scalars] + tuple(
+        pltpu.with_memory_space_constraint(arg, pltpu.VMEM) for arg in args[scalars:]
+    )
+    return pl.pallas_call(
+        body,
+        out_shape=tuple(
+            jax.ShapeDtypeStruct(shape, kind) if index in stored else pltpu.VMEM(shape, kind)
+            for index, (shape, kind) in enumerate(out_shapes)
+        ),
+        in_specs=[SMEM] * scalars + [VMEM] * (len(args) - scalars) + [ANY] * len(after),
+        out_specs=(VMEM,) * len(out_shapes),
+        scratch_shapes=scratch,
+        compiler_params=pltpu.CompilerParams(vmem_limit_bytes=megabytes << 20),
+        name=name,
+    )(*placed, *after)
 
 
 def halves(values):
@@ -78,23 +100,31 @@
     return table
 
 
-def pack_kernel(state_ref, low_ref, high_ref):
+def pack_kernel(band_ref, state_ref, near_ref, far_ref):
+    odd = band_ref[0] % 2
+    near_row = (ROWS - 2) * (1 - odd)
+    far_row = (ROWS - 2) * odd
     for tile in range(N_LON):
-        for place, row in enumerate((0, 1)):
-            low_ref[tile, pl.ds(place * PAIRS, PAIRS), :] = state_ref[
-                tile, pl.ds(row, PAIRS, stride=ROWS), :
-            ]
-        for place, row in enumerate((ROWS - 2, ROWS - 1)):
-            high_ref[tile, pl.ds(place * PAIRS, PAIRS), :] = state_ref[
-                tile, pl.ds(row, PAIRS, stride=ROWS), :
-            ]
-
-
-def stencil(center, east, west, north, south, zonal, meridional, metric):
-    stepped = center - ADVECT * (
-        zonal * metric * (east - west) + meridional * (north - south)
-    )
-    return stepped + DIFFUSE * (east + west + north + south - 4.0 * center)
+        for ref, row in ((near_ref, near_row), (far_ref, far_row)):
+            for place in range(2):
+                ref[tile, pl.ds(place * PAIRS, PAIRS), :] = state_ref[
+                    tile, pl.ds(row + place, PAIRS, stride=ROWS), :
+                ]
+
+
+def weights(zonal, meridional, metric):
+    along = ADVECT * (zonal * metric)
+    across = ADVECT * meridional
+    return DIFFUSE - along, DIFFUSE + along, DIFFUSE - across, DIFFUSE + across
+
+
+def stencil(center, east, west, north, south, shares):
+    to_east, to_west, to_north, to_south = shares
+    return (
+        (1.0 - 4.0 * DIFFUSE) * center
+        + (to_east * east + to_west * west)
+        + (to_north * north + to_south * south)
+    )
 
 
 def turned(field, zonal, meridional, coriolis):
@@ -106,8 +136,8 @@
 
 
 def dynamics_kernel(
-    band_ref, filter_ref, state_ref, north_ref, south_ref, rows_ref, analysis_ref, synthesis_ref,
-    out_ref, stepped_ref, current_ref, split_ref,
+    band_ref, filter_ref, state_ref, near_ref, far_ref, rows_ref, analysis_ref, synthesis_ref,
+    out_ref, north_ref, south_ref, stepped_ref, current_ref, split_ref,
 ):
     band = band_ref[0]
     first = band * ROWS
@@ -116,6 +146,13 @@
     lane_edge = lane[:GROUP]
     metric = rows_ref[band, 0]
     coriolis = rows_ref[band, 1]
+
+    even = lax.broadcasted_iota(jnp.int32, (EDGE, COLS), 0) * 0 + band % 2 == 0
+    for tile in range(N_LON):
+        near_rows = near_ref[tile]
+        far_rows = far_ref[tile]
+        north_ref[tile] = jnp.where(even, near_rows, far_rows)
+        south_ref[tile] = jnp.where(even, far_rows, near_rows)
 
     def beside(load, tile, lanes):
         here = load(tile)
@@ -129,24 +166,25 @@
 
     def step_main(source, north_of, south_of):
         def level_step(level, carry):
-            for field in range(FIELDS):
-                at = pl.ds(pl.multiple_of((field * GROUP + level) * ROWS, ROWS), ROWS)
-                at_u = pl.ds(pl.multiple_of(level * ROWS, ROWS), ROWS)
-                at_v = pl.ds(pl.multiple_of((GROUP + level) * ROWS, ROWS), ROWS)
-                pair = field * GROUP + level
-                for tile in range(N_LON):
-                    here, east, west = beside(lambda t: source[t, at, :], tile, lane)
+            def at(field):
+                return pl.ds(pl.multiple_of((field * GROUP + level) * ROWS, ROWS), ROWS)
+
+            for tile in range(N_LON):
+                zonal = source[tile, at(0), :]
+                meridional = source[tile, at(1), :]
+                shares = weights(zonal, meridional, metric)
+                for field in range(FIELDS):
+                    pair = field * GROUP + level
+                    here, east, west = beside(lambda t: source[t, at(field), :], tile, lane)
                     north = jnp.where(
                         sub == ROWS - 1, north_of(tile, pair), pltpu.roll(here, ROWS - 1, 0)
                     )
                     south = jnp.where(sub == 0, south_of(tile, pair), pltpu.roll(here, 1, 0))
-                    zonal = source[tile, at_u, :]
-                    meridional = source[tile, at_v, :]
-                    result = stencil(here, east, west, north, south, zonal, meridional, metric)
+                    result = stencil(here, east, west, north, south, shares)
                     extra = turned(field, zonal, meridional, coriolis)
                     if extra is not None:
                         result = result + extra
-                    stepped_ref[tile, at, :] = result
+                    stepped_ref[tile, at(field), :] = result
             return carry
 
         lax.fori_loop(0, GROUP, level_step, 0)
@@ -162,6 +200,7 @@
         for tile in range(N_LON):
             zonal = halo[tile, near : near + GROUP, :]
             meridional = halo[tile, near + GROUP : near + 2 * GROUP, :]
+            shares = weights(zonal, meridional, metric_edge)
             for field in range(FIELDS):
                 at = near + field * GROUP
                 here, east, west = beside(lambda t: halo[t, at : at + GROUP, :], tile, lane_edge)
@@ -172,9 +211,7 @@
                     :,
                 ]
                 north, south = ((outer, inner), (inner, outer))[side]
-                result = stencil(
-                    here, east, west, north, south, zonal, meridional, metric_edge
-                )
+                result = stencil(here, east, west, north, south, shares)
                 extra = turned(field, zonal, meridional, coriolis_edge)
                 if extra is not None:
                     result = result + extra
@@ -339,64 +376,57 @@
     analysis, synthesis = (jnp.asarray(table) for table in fourier_tables())
     rows = jnp.asarray(row_tables())
     band = lax.axis_index("lat").astype(jnp.int32).reshape(1)
-    up = [(i, i + 1) for i in range(N_LAT - 1)]
-    down = [(i + 1, i) for i in range(N_LAT - 1)]
-
+
+    state, band = lax.optimization_barrier((state, band))
     by_group = state.reshape(FIELDS, N_LON, GROUP, ROWS, COLS).transpose(1, 0, 2, 3, 4)
     circles = lax.all_to_all(
         by_group.reshape(N_LON, MAIN, COLS), "lon", split_axis=0, concat_axis=0, tiled=True
     )
-    edge = jax.ShapeDtypeStruct((N_LON, EDGE, COLS), F32)
-    first_rows, last_rows = pl.pallas_call(
-        pack_kernel, out_shape=(edge, edge), in_specs=[VMEM], out_specs=(VMEM, VMEM), name="pack"
-    )(circles)
-    north = lax.ppermute(first_rows, "lat", down)
-    south = lax.ppermute(last_rows, "lat", up)
-    dyn = pl.pallas_call(
+    edge = ((N_LON, EDGE, COLS), F32)
+    to_near, to_far = call(pack_kernel, "pack", (edge, edge), [], 4, band, circles, scalars=1)
+    near = lax.ppermute(to_near, "lat", [(i, i ^ 1) for i in range(N_LAT)])
+    far = lax.ppermute(
+        to_far, "lat", [(i, ((i + 1) ^ 1) - 1) for i in range(1, N_LAT - 1)]
+    )
+    levels = ((LEVELS, ROWS, COLS), F32)
+    gain, inverse, order = call(
+        prepare_kernel, "prepare", (levels, levels, ((COLUMNS, COLUMNS), BF16)), [], 4,
+        mixing, block_map,
+        after=(to_near,),
+    )
+    (dyn,) = call(
         dynamics_kernel,
-        out_shape=jax.ShapeDtypeStruct((N_LON, MAIN, COLS), F32),
-        in_specs=[SMEM, SMEM] + [VMEM] * 6,
-        out_specs=VMEM,
-        scratch_shapes=[
+        "dynamics",
+        (((N_LON, MAIN, COLS), F32),),
+        [
+            pltpu.VMEM((N_LON, EDGE, COLS), F32),
+            pltpu.VMEM((N_LON, EDGE, COLS), F32),
             pltpu.VMEM((N_LON, ALL, COLS), F32),
             pltpu.VMEM((N_LON, ALL, COLS), F32),
             pltpu.VMEM((2 * ALL, CIRCLE), BF16),
         ],
-        name="dynamics",
-    )(band, filter_rows, circles, north, south, rows, analysis, synthesis)
-    levels = jax.ShapeDtypeStruct((LEVELS, ROWS, COLS), F32)
-    gain, inverse, order = pl.pallas_call(
-        prepare_kernel,
-        out_shape=(levels, levels, jax.ShapeDtypeStruct((COLUMNS, COLUMNS), BF16)),
-        in_specs=[VMEM] * 2,
-        out_specs=(VMEM,) * 3,
-        name="prepare",
-    )(mixing, block_map)
+        16,
+        band, filter_rows, circles, near, far, rows, analysis, synthesis,
+        scalars=2,
+        after=(gain,),
+    )
     columns = lax.all_to_all(dyn, "lon", split_axis=0, concat_axis=0, tiled=True)
-    new_state, sent = pl.pallas_call(
+    new_state, sent = call(
         physics_kernel,
-        out_shape=(
-            jax.ShapeDtypeStruct((FIELDS, LEVELS, ROWS, COLS), F32),
-            jax.ShapeDtypeStruct((COLUMNS, COLS), F32),
-        ),
-        in_specs=[VMEM] * 7,
-        out_specs=(VMEM,) * 2,
-        scratch_shapes=[
-            pltpu.VMEM((LEVELS * ROWS, COLS), F32),
-            pltpu.VMEM((2 * COLS, COLUMNS), BF16),
-        ],
-        name="physics",
-    )(columns, mixing, insolation, block_map, gain, inverse, order)
+        "physics",
+        (((FIELDS, LEVELS, ROWS, COLS), F32), ((COLUMNS, COLS), F32)),
+        [pltpu.VMEM((LEVELS * ROWS, COLS), F32), pltpu.VMEM((2 * COLS, COLUMNS), BF16)],
+        12,
+        columns, mixing, insolation, block_map, gain, inverse, order,
+        stored=(),
+    )
     got = lax.all_to_all(
         sent.reshape(BLOCKS, ROWS, COLS), ("lat", "lon"), split_axis=0, concat_axis=0, tiled=True
     )
-    block_heating = pl.pallas_call(
-        place_kernel,
-        out_shape=jax.ShapeDtypeStruct((1, LEVELS, COLUMNS), F32),
-        in_specs=[VMEM],
-        out_specs=VMEM,
-        name="place",
-    )(got.reshape(COLUMNS, COLS))
+    (block_heating,) = call(
+        place_kernel, "place", (((1, LEVELS, COLUMNS), F32),), [], 8, got.reshape(COLUMNS, COLS),
+        stored=(0,),
+    )
     return new_state, block_heating
 
 

time: 106 us -> 94.3 us (0.89)
  Pallas kernels: 24.1 us -> 14.2 us
  waiting for transfers between devices: 17.2 us -> 14.3 us
  starting transfers between devices: 10.4 us -> 12.3 us
    pallas_call x5, Pallas kernels: 24.1 us -> 14.2 us  [call(): pl.pallas_call(body, out_shape=tuple((jax.ShapeDtypeStruct(shape, kind) i...]
    all_to_all x1, starting transfers between devices: 3.7 us -> 7.28 us  [per_device(): lax.all_to_all(sent.reshape(BLOCKS, ROWS, COLS), ('lat', 'lon'), split_ax...]
    ppermute x2, waiting for transfers between devices: 4.31 us -> 1.97 us  [the longest x1 1.97 us: per_device(): lax.ppermute(to_far, 'lat', [(i, (i + 1 ^ 1) - 1) for i in range(1, N_LAT...]
    ppermute x2, starting transfers between devices: 6.74 us -> 5.05 us  [the longest x1 4.96 us: per_device(): lax.ppermute(to_far, 'lat', [(i, (i + 1 ^ 1) - 1) for i in range(1, N_LAT...]
  transfers between devices with their start and end apart: 3 -> 3, of which waited for: 3 -> 2; matrix products, arithmetic and copies ran while one was open for 0% -> 1% of each run, Pallas kernels for 4% -> 3%
where the time goes in v1:
time: 94.3 us; the launch traced here: 94 us
  blocking collectives  49.9 us (53%)
  waiting for transfers between devices  14.3 us (15%)
  Pallas kernels  14.2 us (15%)
  starting transfers between devices  12.3 us (13%)
  local copies, waits for them, and re-layouts  2.53 us (3%)
    all_to_all x1, blocking collectives, per_device(): lax.all_to_all(by_group.reshape(N_LON, MAIN, COLS), 'lon', split_axis=0,...  27.3 us
    all_to_all x1, blocking collectives, per_device(): lax.all_to_all(dyn, 'lon', split_axis=0, concat_axis=0, tiled=True)  22.6 us
    pallas_call x5, Pallas kernels, call(): pl.pallas_call(body, out_shape=tuple((jax.ShapeDtypeStruct(shape, kind) i...  14.2 us
    all_to_all x1, waiting for transfers between devices, per_device(): lax.all_to_all(sent.reshape(BLOCKS, ROWS, COLS), ('lat', 'lon'), split_ax...  12.4 us
    all_to_all x1, starting transfers between devices, per_device(): lax.all_to_all(sent.reshape(BLOCKS, ROWS, COLS), ('lat', 'lon'), split_ax...  7.28 us
    ppermute x1, starting transfers between devices, per_device(): lax.ppermute(to_far, 'lat', [(i, (i + 1 ^ 1) - 1) for i in range(1, N_LAT...  4.96 us
    ppermute x1, waiting for transfers between devices, per_device(): lax.ppermute(to_far, 'lat', [(i, (i + 1 ^ 1) - 1) for i in range(1, N_LAT...  1.97 us
  transfers between devices with their start and end apart: 3, of which 2 were waited for; matrix products, arithmetic and copies ran while one was open for 1% of the time, Pallas kernels for 3%

profile of v1, /device:TPU:1, one launch (start us, length us, event | category | flops | bytes accessed | tf_op | source)
XLA Modules:
  0.0 94.0 jit_solution(4618078783763019910)
XLA Ops:
  0.6 1.4 %copy.10 = f32[4,16,5,8,128]{4,3,2,0,1:T(8,128)S(1)} copy(f32[4,16,5,8,128]{4,3,2,1,0:T(8,128)} %bitcast.9) | data formatting | bytes 2621440 | tf_op jit(solution)/shard_map/reshape | solution.py:381
  2.1 0.0 copy-start.4
  2.1 0.0 copy-start.1
  2.1 27.3 %all_to_all.15.refs_1_.refs_2_ = f32[16,160,128]{2,1,0:T(8,128)S(1)} all-to-all(f32[16,160,128]{2,1,0:T(8,128)S(1)} %bitcast.8), channel_id=1, replica_groups=mesh['lat'=8,'lon'=16] {'lon'}, dimensions={0} | all-to-all | bytes 2621440 | tf_op jit(solution)/shard_map/all_to_all | solution.py:382
  29.4 0.0 copy-start.3
  29.4 0.0 copy-start
  29.4 0.0 copy-start.2
  29.4 0.0 copy-start.6
  29.4 0.1 pack.1
  29.6 5.0 %collective-permute-start.1 = (f32[16,40,128]{2,1,0:T(8,128)S(1)}, f32[16,40,128]{2,1,0:T(8,128)S(1)}, u32[]{:S(2)}, u32[]{:S(2)}) collective-permute-start(f32[16,40,128]{2,1,0:T(8,128)S(1)} %get-tuple-element.14), channel_id=1, source_target_pairs={{16,32},{32,16},{48,64},{64,48},{80,96},{96,80},{17,33},{33,17},{4... | collective-permute-start | bytes 983048 | tf_op jit(solution)/shard_map/ppermute | solution.py:388
  34.5 0.1 collective-permute-start
  34.6 0.0 copy-done.4
  34.6 0.0 copy-done.3
  34.6 2.7 %prepare.1 = (f32[80,8,128]{2,1,0:T(8,128)S(1)}, f32[80,8,128]{2,1,0:T(8,128)S(1)}, bf16[1024,1024]{1,0:T(8,128)(2,1)S(1)}) custom-call(f32[8,128]{1,0:T(8,128)S(1)} %copy-done.3, s32[8,128]{1,0:T(8,128)S(1)} %copy-done.4, f32[16,40,128]{2,1,0:T(8,128)S(1)} %get-tuple-element.13.refs_2_), custom_call_target="tpu_custom_call" | custom-call | tf_op jit(solution)/shard_map/prepare/pallas_call | solution.py:48
  37.3 2.0 %collective-permute-done.1.refs_4_ = f32[16,40,128]{2,1,0:T(8,128)S(1)} collective-permute-done((f32[16,40,128]{2,1,0:T(8,128)S(1)}, f32[16,40,128]{2,1,0:T(8,128)S(1)}, u32[]{:S(2)}, u32[]{:S(2)}) %collective-permute-start.1) | collective-permute-done | bytes 327712 | tf_op jit(solution)/shard_map/ppermute | solution.py:388
  39.3 0.0 collective-permute-done.refs_3_
  39.3 0.0 copy-done.1
  39.3 0.0 copy-done
  39.3 0.0 copy-done.2
  39.3 0.0 copy-done.6
  39.3 7.8 %dynamics.1 = f32[16,160,128]{2,1,0:T(8,128)S(1)} custom-call(s32[1]{0:T(128)} %bitcast.refs_0_, s32[64]{0:T(128)S(1)} %copy-done.6, f32[16,160,128]{2,1,0:T(8,128)S(1)} %all_to_all.15.refs_1_.refs_2_, f32[16,40,128]{2,1,0:T(8,128)S(1)} %collective-permute-done.refs_3_, f32[16,40,128]{2,1,0:T(8,128)S(1)} %collective-permute-done.1.refs_4_, ...), custom_call_target="tpu_custom_call" | custom-call | tf_op jit(solution)/shard_map/dynamics/pallas_call | solution.py:48
  47.1 0.0 copy-start.5
  47.1 22.6 %all_to_all.16.refs_0_ = f32[16,160,128]{2,1,0:T(8,128)S(1)} all-to-all(f32[16,160,128]{2,1,0:T(8,128)S(1)} %dynamics.1), channel_id=1, replica_groups=mesh['lat'=8,'lon'=16] {'lon'}, dimensions={0} | all-to-all | bytes 2621440 | tf_op jit(solution)/shard_map/all_to_all | solution.py:413
  69.7 0.0 copy-done.5
  69.7 2.2 %physics.1 = (f32[4,80,8,128]{3,2,1,0:T(8,128)S(1)}, f32[1024,128]{1,0:T(8,128)}) custom-call(f32[16,160,128]{2,1,0:T(8,128)S(1)} %all_to_all.16.refs_0_, f32[8,128]{1,0:T(8,128)S(1)} %copy-done.3, f32[8,128]{1,0:T(8,128)S(1)} %copy-done.5, s32[8,128]{1,0:T(8,128)S(1)} %copy-done.4, f32[80,8,128]{2,1,0:T(8,128)S(1)} %get-tuple-element.15.refs_8_.refs_4_, ...), custom_call_target="tpu_custom_call" | custom-call | tf_op jit(solution)/shard_map/physics/pallas_call | solution.py:48
  71.8 7.3 %all-to-all-start.2 = ((f32[128,8,128]{2,1,0:T(8,128)}), f32[128,8,128]{2,1,0:T(8,128)S(1)}, u32[]{:S(2)}, u32[]{:S(2)}) async-start(f32[128,8,128]{2,1,0:T(8,128)} %bitcast.4), calls=%async_computation.2 | async-start | bytes 1048576 | tf_op jit(solution)/shard_map/all_to_all | solution.py:423
  79.1 1.1 %copy.11 = f32[4,80,8,128]{3,2,1,0:T(8,128)} copy(f32[4,80,8,128]{3,2,1,0:T(8,128)S(1)} %get-tuple-element.20) | data formatting | bytes 2621440
  80.2 12.4 %all-to-all-done.2 = f32[128,8,128]{2,1,0:T(8,128)S(1)} async-done(((f32[128,8,128]{2,1,0:T(8,128)}), f32[128,8,128]{2,1,0:T(8,128)S(1)}, u32[]{:S(2)}, u32[]{:S(2)}) %all-to-all-start.2) | async-done | bytes 524320 | tf_op jit(solution)/shard_map/all_to_all | solution.py:423
  92.6 1.4 %place.1 = f32[1,80,1024]{2,1,0:T(8,128)} custom-call(f32[1024,128]{1,0:T(8,128)S(1)} %bitcast.7), custom_call_target="tpu_custom_call" | custom-call | tf_op jit(solution)/shard_map/place/pallas_call | solution.py:48
Async XLA Ops:
  2.1 32.5 %copy-start.4 = (s32[8,128]{1,0:T(8,128)S(1)}, s32[8,128]{1,0:T(8,128)}, u32[]{:S(2)}) copy-start(s32[8,128]{1,0:T(8,128)} %refs_3_.1) | copy-start | bytes 12292
  2.1 37.2 %copy-start.1 = (bf16[2048,256]{1,0:T(8,128)(2,1)S(1)}, bf16[2048,256]{1,0:T(8,128)(2,1)}, u32[]{:S(2)}) copy-start(bf16[2048,256]{1,0:T(8,128)(2,1)} %constant.12.clone.refs_6_) | copy-start | bytes 3145732
  29.4 5.2 %copy-start.3 = (f32[8,128]{1,0:T(8,128)S(1)}, f32[8,128]{1,0:T(8,128)}, u32[]{:S(2)}) copy-start(f32[8,128]{1,0:T(8,128)} %refs_1_.5) | copy-start | bytes 12292
  29.4 9.9 %copy-start = (bf16[256,2048]{1,0:T(8,128)(2,1)S(1)}, bf16[256,2048]{1,0:T(8,128)(2,1)}, u32[]{:S(2)}) copy-start(bf16[256,2048]{1,0:T(8,128)(2,1)} %constant.13.clone.refs_7_) | copy-start | bytes 3145732
  29.4 9.9 %copy-start.2 = (f32[8,8,8,128]{3,2,1,0:T(8,128)S(1)}, f32[8,8,8,128]{3,2,1,0:T(8,128)}, u32[]{:S(2)}) copy-start(f32[8,8,8,128]{3,2,1,0:T(8,128)} %constant.14.clone.refs_5_) | copy-start | bytes 786436
  29.4 9.9 %copy-start.6 = (s32[64]{0:T(128)S(1)}, s32[64]{0:T(128)}, u32[]{:S(2)}) copy-start(s32[64]{0:T(128)} %refs_1_.4) | copy-start | bytes 772
  29.6 9.7 %collective-permute-start.1 = (f32[16,40,128]{2,1,0:T(8,128)S(1)}, f32[16,40,128]{2,1,0:T(8,128)S(1)}, u32[]{:S(2)}, u32[]{:S(2)}) collective-permute-start(f32[16,40,128]{2,1,0:T(8,128)S(1)} %get-tuple-element.14), channel_id=1, source_target_pairs={{16,32},{32,16},{48,64},{64,48},{80,96},{96,80},{17,33},{33,17},{4... | collective-permute-start | bytes 983048 | tf_op jit(solution)/shard_map/ppermute | solution.py:388
  34.5 4.7 %collective-permute-start = (f32[16,40,128]{2,1,0:T(8,128)S(1)}, f32[16,40,128]{2,1,0:T(8,128)S(1)}, u32[]{:S(2)}, u32[]{:S(2)}) collective-permute-start(f32[16,40,128]{2,1,0:T(8,128)S(1)} %get-tuple-element.13.refs_2_), channel_id=1, source_target_pairs={{0,16},{16,0},{32,48},{48,32},{64,80},{80,64},{96,112},{112,96},{1... | collective-permute-start | bytes 983048 | tf_op jit(solution)/shard_map/ppermute | solution.py:387
  47.1 22.6 %copy-start.5 = (f32[8,128]{1,0:T(8,128)S(1)}, f32[8,128]{1,0:T(8,128)}, u32[]{:S(2)}) copy-start(f32[8,128]{1,0:T(8,128)} %refs_2_.1) | copy-start | bytes 12292
  71.8 20.7 %all-to-all-start.2 = ((f32[128,8,128]{2,1,0:T(8,128)}), f32[128,8,128]{2,1,0:T(8,128)S(1)}, u32[]{:S(2)}, u32[]{:S(2)}) async-start(f32[128,8,128]{2,1,0:T(8,128)} %bitcast.4), calls=%async_computation.2 | async-start | bytes 1048576 | tf_op jit(solution)/shard_map/all_to_all | solution.py:423

commit v2 on v1

--- a/solution.py
+++ b/solution.py
@@ -135,15 +135,79 @@
     return None
 
 
+def neighbours(load, lanes):
+    kept = {}
+
+    def rolled(tile, shift):
+        tile = tile % N_LON
+        if (tile, shift) not in kept:
+            kept[tile, shift] = pltpu.roll(load(tile), shift, 1)
+        return kept[tile, shift]
+
+    def beside(tile):
+        east = jnp.where(lanes == COLS - 1, rolled(tile + 1, COLS - 1), rolled(tile, COLS - 1))
+        west = jnp.where(lanes == 0, rolled(tile - 1, 1), rolled(tile, 1))
+        return load(tile), east, west
+
+    return beside
+
+
+def step_main(source, target, north_of, south_of, metric, coriolis):
+    lane = lax.broadcasted_iota(jnp.int32, (ROWS, COLS), 1)
+    sub = lax.broadcasted_iota(jnp.int32, (ROWS, COLS), 0)
+
+    def level_step(level, carry):
+        def at(field):
+            return pl.ds(pl.multiple_of((field * GROUP + level) * ROWS, ROWS), ROWS)
+
+        def reader(field):
+            kept = {}
+
+            def load(tile):
+                if tile not in kept:
+                    kept[tile] = source[tile, at(field), :]
+                return kept[tile]
+
+            return load
+
+        beside = [neighbours(reader(field), lane) for field in range(FIELDS)]
+        for tile in range(N_LON):
+            zonal = source[tile, at(0), :]
+            meridional = source[tile, at(1), :]
+            shares = weights(zonal, meridional, metric)
+            for field in range(FIELDS):
+                pair = field * GROUP + level
+                here, east, west = beside[field](tile)
+                north = jnp.where(
+                    sub == ROWS - 1, north_of(tile, pair), pltpu.roll(here, ROWS - 1, 0)
+                )
+                south = jnp.where(sub == 0, south_of(tile, pair), pltpu.roll(here, 1, 0))
+                result = stencil(here, east, west, north, south, shares)
+                extra = turned(field, zonal, meridional, coriolis)
+                if extra is not None:
+                    result = result + extra
+                target[tile, at(field), :] = result
+        return carry
+
+    lax.fori_loop(0, GROUP, level_step, 0)
+
+
+def inside_kernel(band_ref, state_ref, rows_ref, out_ref):
+    band = band_ref[0]
+    step_main(
+        state_ref, out_ref, lambda tile, pair: 0.0, lambda tile, pair: 0.0,
+        rows_ref[band, 0], rows_ref[band, 1],
+    )
+
+
 def dynamics_kernel(
-    band_ref, filter_ref, state_ref, near_ref, far_ref, rows_ref, analysis_ref, synthesis_ref,
+    band_ref, filter_ref, state_ref, inside_ref, near_ref, far_ref, rows_ref, analysis_ref, synthesis_ref,
     out_ref, north_ref, south_ref, stepped_ref, current_ref, split_ref,
 ):
     band = band_ref[0]
     first = band * ROWS
-    lane = lax.broadcasted_iota(jnp.int32, (ROWS, COLS), 1)
     sub = lax.broadcasted_iota(jnp.int32, (ROWS, COLS), 0)
-    lane_edge = lane[:GROUP]
+    lane_edge = lax.broadcasted_iota(jnp.int32, (GROUP, COLS), 1)
     metric = rows_ref[band, 0]
     coriolis = rows_ref[band, 1]
 
@@ -153,41 +217,6 @@
         far_rows = far_ref[tile]
         north_ref[tile] = jnp.where(even, near_rows, far_rows)
         south_ref[tile] = jnp.where(even, far_rows, near_rows)
-
-    def beside(load, tile, lanes):
-        here = load(tile)
-        after = load((tile + 1) % N_LON)
-        before = load((tile - 1) % N_LON)
-        east = jnp.where(
-            lanes == COLS - 1, pltpu.roll(after, COLS - 1, 1), pltpu.roll(here, COLS - 1, 1)
-        )
-        west = jnp.where(lanes == 0, pltpu.roll(before, 1, 1), pltpu.roll(here, 1, 1))
-        return here, east, west
-
-    def step_main(source, north_of, south_of):
-        def level_step(level, carry):
-            def at(field):
-                return pl.ds(pl.multiple_of((field * GROUP + level) * ROWS, ROWS), ROWS)
-
-            for tile in range(N_LON):
-                zonal = source[tile, at(0), :]
-                meridional = source[tile, at(1), :]
-                shares = weights(zonal, meridional, metric)
-                for field in range(FIELDS):
-                    pair = field * GROUP + level
-                    here, east, west = beside(lambda t: source[t, at(field), :], tile, lane)
-                    north = jnp.where(
-                        sub == ROWS - 1, north_of(tile, pair), pltpu.roll(here, ROWS - 1, 0)
-                    )
-                    south = jnp.where(sub == 0, south_of(tile, pair), pltpu.roll(here, 1, 0))
-                    result = stencil(here, east, west, north, south, shares)
-                    extra = turned(field, zonal, meridional, coriolis)
-                    if extra is not None:
-                        result = result + extra
-                    stepped_ref[tile, at(field), :] = result
-            return carry
-
-        lax.fori_loop(0, GROUP, level_step, 0)
 
     def step_edge(side):
         base = 2 + 3 * side
@@ -197,19 +226,24 @@
         halo = (north_ref, south_ref)[side]
         near = (0, PAIRS)[side]
         far = (PAIRS, 0)[side]
+        own = (ROWS - 1, 0)[side]
+        beside = [
+            neighbours(
+                lambda t, at=near + field * GROUP: halo[t, at : at + GROUP, :], lane_edge
+            )
+            for field in range(FIELDS)
+        ]
         for tile in range(N_LON):
             zonal = halo[tile, near : near + GROUP, :]
             meridional = halo[tile, near + GROUP : near + 2 * GROUP, :]
             shares = weights(zonal, meridional, metric_edge)
+            own_wind = state_ref[tile, pl.ds(GROUP * ROWS + own, GROUP, stride=ROWS), :]
+            given = DIFFUSE + (-ADVECT, ADVECT)[side] * own_wind
             for field in range(FIELDS):
-                at = near + field * GROUP
-                here, east, west = beside(lambda t: halo[t, at : at + GROUP, :], tile, lane_edge)
+                own_rows = pl.ds(field * GROUP * ROWS + own, GROUP, stride=ROWS)
+                here, east, west = beside[field](tile)
                 outer = halo[tile, far + field * GROUP : far + (field + 1) * GROUP, :]
-                inner = state_ref[
-                    tile,
-                    pl.ds(field * GROUP * ROWS + (ROWS - 1, 0)[side], GROUP, stride=ROWS),
-                    :,
-                ]
+                inner = state_ref[tile, own_rows, :]
                 north, south = ((outer, inner), (inner, outer))[side]
                 result = stencil(here, east, west, north, south, shares)
                 extra = turned(field, zonal, meridional, coriolis_edge)
@@ -217,6 +251,7 @@
                     result = result + extra
                 place = MAIN + side * PAIRS + field * GROUP
                 stepped_ref[tile, place : place + GROUP, :] = jnp.where(exists > 0.5, result, 0.0)
+                stepped_ref[tile, own_rows, :] = stepped_ref[tile, own_rows, :] + given * here
 
     wanted = jnp.zeros((ROWS, COLS), jnp.int32)
     for row in range(ROWS):
@@ -258,18 +293,18 @@
                     )
 
     stepped_ref[:, MAIN + EDGE :, :] = jnp.zeros((N_LON, ALL - MAIN - EDGE, COLS), F32)
-    step_main(
-        state_ref,
-        lambda tile, pair: north_ref[tile, pl.ds(pair, 1), :],
-        lambda tile, pair: south_ref[tile, pl.ds(PAIRS + pair, 1), :],
-    )
+    for tile in range(N_LON):
+        stepped_ref[tile, :MAIN, :] = inside_ref[tile]
     step_edge(0)
     step_edge(1)
     polar_filter(ALL, current_ref)
     step_main(
         current_ref,
+        stepped_ref,
         lambda tile, pair: current_ref[tile, pl.ds(MAIN + pair, 1), :],
         lambda tile, pair: current_ref[tile, pl.ds(MAIN + PAIRS + pair, 1), :],
+        metric,
+        coriolis,
     )
     polar_filter(MAIN, out_ref)
 
@@ -388,6 +423,10 @@
     far = lax.ppermute(
         to_far, "lat", [(i, ((i + 1) ^ 1) - 1) for i in range(1, N_LAT - 1)]
     )
+    (inside,) = call(
+        inside_kernel, "inside", (((N_LON, MAIN, COLS), F32),), [], 4, band, circles, rows,
+        scalars=1, after=(to_near, to_far),
+    )
     levels = ((LEVELS, ROWS, COLS), F32)
     gain, inverse, order = call(
         prepare_kernel, "prepare", (levels, levels, ((COLUMNS, COLUMNS), BF16)), [], 4,
@@ -406,7 +445,7 @@
             pltpu.VMEM((2 * ALL, CIRCLE), BF16),
         ],
         16,
-        band, filter_rows, circles, near, far, rows, analysis, synthesis,
+        band, filter_rows, circles, inside, near, far, rows, analysis, synthesis,
         scalars=2,
         after=(gain,),
     )

time: 94.3 us -> 92.1 us (0.977)
  waiting for transfers between devices: 14.3 us -> 13.2 us
    ppermute x1, waiting for transfers between devices: 1.97 us -> 0.78 us  [per_device(): lax.ppermute(to_far, 'lat', [(i, (i + 1 ^ 1) - 1) for i in range(1, N_LAT...]
    pallas_call x5 -> x6, Pallas kernels: 14.2 us -> 13.4 us  [call(): pl.pallas_call(body, out_shape=tuple((jax.ShapeDtypeStruct(shape, kind) i...]
  transfers between devices with their start and end apart: 3 -> 3, of which waited for: 2 -> 2; matrix products, arithmetic and copies ran while one was open for 1% -> 1% of each run, Pallas kernels for 3% -> 4%
where the time goes in v2:
time: 92.1 us; the launch traced here: 91.8 us
  blocking collectives  49.5 us (54%)
  Pallas kernels  13.4 us (15%)
  waiting for transfers between devices  13.2 us (14%)
  starting transfers between devices  12.4 us (13%)
  local copies, waits for them, and re-layouts  2.54 us (3%)
    all_to_all x1, blocking collectives, per_device(): lax.all_to_all(by_group.reshape(N_LON, MAIN, COLS), 'lon', split_axis=0,...  27.2 us
    all_to_all x1, blocking collectives, per_device(): lax.all_to_all(dyn, 'lon', split_axis=0, concat_axis=0, tiled=True)  22.4 us
    pallas_call x6, Pallas kernels, call(): pl.pallas_call(body, out_shape=tuple((jax.ShapeDtypeStruct(shape, kind) i...  13.4 us
    all_to_all x1, waiting for transfers between devices, per_device(): lax.all_to_all(sent.reshape(BLOCKS, ROWS, COLS), ('lat', 'lon'), split_ax...  12.4 us
    all_to_all x1, starting transfers between devices, per_device(): lax.all_to_all(sent.reshape(BLOCKS, ROWS, COLS), ('lat', 'lon'), split_ax...  7.49 us
    ppermute x1, starting transfers between devices, per_device(): lax.ppermute(to_far, 'lat', [(i, (i + 1 ^ 1) - 1) for i in range(1, N_LAT...  4.83 us
  transfers between devices with their start and end apart: 3, of which 2 were waited for; matrix products, arithmetic and copies ran while one was open for 1% of the time, Pallas kernels for 4%

profile of v2, /device:TPU:1, one launch (start us, length us, event | category | flops | bytes accessed | tf_op | source)
XLA Modules:
  0.0 91.8 jit_solution(3508964737380491646)
XLA Ops:
  0.6 1.4 %copy.10 = f32[4,16,5,8,128]{4,3,2,0,1:T(8,128)S(1)} copy(f32[4,16,5,8,128]{4,3,2,1,0:T(8,128)} %bitcast.9) | data formatting | bytes 2621440 | tf_op jit(solution)/shard_map/reshape | solution.py:416
  2.1 27.2 %all_to_all.15.refs_1_.refs_2_ = f32[16,160,128]{2,1,0:T(8,128)S(1)} all-to-all(f32[16,160,128]{2,1,0:T(8,128)S(1)} %bitcast.8), channel_id=1, replica_groups=mesh['lat'=8,'lon'=16] {'lon'}, dimensions={0} | all-to-all | bytes 2621440 | tf_op jit(solution)/shard_map/all_to_all | solution.py:417
  29.3 0.0 copy-start.3
  29.3 0.0 copy-start.4
  29.3 0.0 copy-start
  29.3 0.1 pack.1
  29.4 4.8 %collective-permute-start.1 = (f32[16,40,128]{2,1,0:T(8,128)S(1)}, f32[16,40,128]{2,1,0:T(8,128)S(1)}, u32[]{:S(2)}, u32[]{:S(2)}) collective-permute-start(f32[16,40,128]{2,1,0:T(8,128)S(1)} %get-tuple-element.14.refs_4_), channel_id=1, source_target_pairs={{16,32},{32,16},{48,64},{64,48},{80,96},{96,80},{17,33},{33,17},{4... | collective-permute-start | bytes 983048 | tf_op jit(solution)/shard_map/ppermute | solution.py:423
  34.2 0.1 collective-permute-start
  34.3 0.0 copy-done.3
  34.3 0.0 copy-done.4
  34.3 2.7 %prepare.1 = (f32[80,8,128]{2,1,0:T(8,128)S(1)}, f32[80,8,128]{2,1,0:T(8,128)S(1)}, bf16[1024,1024]{1,0:T(8,128)(2,1)S(1)}) custom-call(f32[8,128]{1,0:T(8,128)S(1)} %copy-done.3, s32[8,128]{1,0:T(8,128)S(1)} %copy-done.4, f32[16,40,128]{2,1,0:T(8,128)S(1)} %get-tuple-element.13.refs_3_.refs_2_), custom_call_target="tpu_custom_call" | custom-call | tf_op jit(solution)/shard_map/prepare/pallas_call | solution.py:48
  37.0 0.0 copy-done
  37.0 0.0 copy-start.1
  37.0 0.0 copy-start.2
  37.0 0.0 copy-start.6
  37.1 1.1 %inside.1.refs_3_ = f32[16,160,128]{2,1,0:T(8,128)S(1)} custom-call(s32[1]{0:T(128)} %bitcast.refs_0_, f32[16,160,128]{2,1,0:T(8,128)S(1)} %all_to_all.15.refs_1_.refs_2_, f32[8,8,8,128]{3,2,1,0:T(8,128)S(1)} %copy-done, f32[16,40,128]{2,1,0:T(8,128)S(1)} %get-tuple-element.13.refs_3_.refs_2_, f32[16,40,128]{2,1,0:T(8,128)S(1)} %get-tuple-element.14.refs_4_), custom_call_target="tpu_custom_call" | custom-call | tf_op jit(solution)/shard_map/inside/pallas_call | solution.py:48
  38.2 0.8 collective-permute-done.1.refs_5_
  39.0 0.0 collective-permute-done.refs_4_
  39.0 0.0 copy-done.1
  39.0 0.0 copy-done.2
  39.0 0.0 copy-done.6
  39.0 5.9 %dynamics.1 = f32[16,160,128]{2,1,0:T(8,128)S(1)} custom-call(s32[1]{0:T(128)} %bitcast.refs_0_, s32[64]{0:T(128)S(1)} %copy-done.6, f32[16,160,128]{2,1,0:T(8,128)S(1)} %all_to_all.15.refs_1_.refs_2_, f32[16,160,128]{2,1,0:T(8,128)S(1)} %inside.1.refs_3_, f32[16,40,128]{2,1,0:T(8,128)S(1)} %collective-permute-done.refs_4_, ...), custom_call_target="tpu_custom_call" | custom-call | tf_op jit(solution)/shard_map/dynamics/pallas_call | solution.py:48
  44.9 0.0 copy-start.5
  44.9 22.4 %all_to_all.16.refs_0_ = f32[16,160,128]{2,1,0:T(8,128)S(1)} all-to-all(f32[16,160,128]{2,1,0:T(8,128)S(1)} %dynamics.1), channel_id=1, replica_groups=mesh['lat'=8,'lon'=16] {'lon'}, dimensions={0} | all-to-all | bytes 2621440 | tf_op jit(solution)/shard_map/all_to_all | solution.py:452
  67.2 0.0 copy-done.5
  67.2 2.1 %physics.1 = (f32[4,80,8,128]{3,2,1,0:T(8,128)S(1)}, f32[1024,128]{1,0:T(8,128)}) custom-call(f32[16,160,128]{2,1,0:T(8,128)S(1)} %all_to_all.16.refs_0_, f32[8,128]{1,0:T(8,128)S(1)} %copy-done.3, f32[8,128]{1,0:T(8,128)S(1)} %copy-done.5, s32[8,128]{1,0:T(8,128)S(1)} %copy-done.4, f32[80,8,128]{2,1,0:T(8,128)S(1)} %get-tuple-element.15.refs_9_.refs_4_, ...), custom_call_target="tpu_custom_call" | custom-call | tf_op jit(solution)/shard_map/physics/pallas_call | solution.py:48
  69.4 7.5 %all-to-all-start.2 = ((f32[128,8,128]{2,1,0:T(8,128)}), f32[128,8,128]{2,1,0:T(8,128)S(1)}, u32[]{:S(2)}, u32[]{:S(2)}) async-start(f32[128,8,128]{2,1,0:T(8,128)} %bitcast.4), calls=%async_computation.2 | async-start | bytes 1048576 | tf_op jit(solution)/shard_map/all_to_all | solution.py:462
  76.9 1.1 %copy.11 = f32[4,80,8,128]{3,2,1,0:T(8,128)} copy(f32[4,80,8,128]{3,2,1,0:T(8,128)S(1)} %get-tuple-element.20) | data formatting | bytes 2621440
  78.0 12.4 %all-to-all-done.2 = f32[128,8,128]{2,1,0:T(8,128)S(1)} async-done(((f32[128,8,128]{2,1,0:T(8,128)}), f32[128,8,128]{2,1,0:T(8,128)S(1)}, u32[]{:S(2)}, u32[]{:S(2)}) %all-to-all-start.2) | async-done | bytes 524320 | tf_op jit(solution)/shard_map/all_to_all | solution.py:462
  90.3 1.4 %place.1 = f32[1,80,1024]{2,1,0:T(8,128)} custom-call(f32[1024,128]{1,0:T(8,128)S(1)} %bitcast.7), custom_call_target="tpu_custom_call" | custom-call | tf_op jit(solution)/shard_map/place/pallas_call | solution.py:48
Async XLA Ops:
  29.3 5.1 %copy-start.3 = (f32[8,128]{1,0:T(8,128)S(1)}, f32[8,128]{1,0:T(8,128)}, u32[]{:S(2)}) copy-start(f32[8,128]{1,0:T(8,128)} %refs_1_.5) | copy-start | bytes 12292
  29.3 5.1 %copy-start.4 = (s32[8,128]{1,0:T(8,128)S(1)}, s32[8,128]{1,0:T(8,128)}, u32[]{:S(2)}) copy-start(s32[8,128]{1,0:T(8,128)} %refs_3_.1) | copy-start | bytes 12292
  29.3 7.7 %copy-start = (f32[8,8,8,128]{3,2,1,0:T(8,128)S(1)}, f32[8,8,8,128]{3,2,1,0:T(8,128)}, u32[]{:S(2)}) copy-start(f32[8,8,8,128]{3,2,1,0:T(8,128)} %constant.14.clone.refs_2_.refs_6_) | copy-start | bytes 786436
  29.4 9.6 %collective-permute-start.1 = (f32[16,40,128]{2,1,0:T(8,128)S(1)}, f32[16,40,128]{2,1,0:T(8,128)S(1)}, u32[]{:S(2)}, u32[]{:S(2)}) collective-permute-start(f32[16,40,128]{2,1,0:T(8,128)S(1)} %get-tuple-element.14.refs_4_), channel_id=1, source_target_pairs={{16,32},{32,16},{48,64},{64,48},{80,96},{96,80},{17,33},{33,17},{4... | collective-permute-start | bytes 983048 | tf_op jit(solution)/shard_map/ppermute | solution.py:423
  34.2 4.7 %collective-permute-start = (f32[16,40,128]{2,1,0:T(8,128)S(1)}, f32[16,40,128]{2,1,0:T(8,128)S(1)}, u32[]{:S(2)}, u32[]{:S(2)}) collective-permute-start(f32[16,40,128]{2,1,0:T(8,128)S(1)} %get-tuple-element.13.refs_3_.refs_2_), channel_id=1, source_target_pairs={{0,16},{16,0},{32,48},{48,32},{64,80},{80,64},{96,112},{112,96},{1... | collective-permute-start | bytes 983048 | tf_op jit(solution)/shard_map/ppermute | solution.py:422
  37.0 2.0 %copy-start.1 = (bf16[256,2048]{1,0:T(8,128)(2,1)S(1)}, bf16[256,2048]{1,0:T(8,128)(2,1)}, u32[]{:S(2)}) copy-start(bf16[256,2048]{1,0:T(8,128)(2,1)} %constant.13.clone.refs_8_) | copy-start | bytes 3145732
  37.0 2.0 %copy-start.2 = (bf16[2048,256]{1,0:T(8,128)(2,1)S(1)}, bf16[2048,256]{1,0:T(8,128)(2,1)}, u32[]{:S(2)}) copy-start(bf16[2048,256]{1,0:T(8,128)(2,1)} %constant.12.clone.refs_7_) | copy-start | bytes 3145732
  37.0 1.9 %copy-start.6 = (s32[64]{0:T(128)S(1)}, s32[64]{0:T(128)}, u32[]{:S(2)}) copy-start(s32[64]{0:T(128)} %refs_1_.4) | copy-start | bytes 772
  44.9 22.4 %copy-start.5 = (f32[8,128]{1,0:T(8,128)S(1)}, f32[8,128]{1,0:T(8,128)}, u32[]{:S(2)}) copy-start(f32[8,128]{1,0:T(8,128)} %refs_2_.2) | copy-start | bytes 12292
  69.4 20.9 %all-to-all-start.2 = ((f32[128,8,128]{2,1,0:T(8,128)}), f32[128,8,128]{2,1,0:T(8,128)S(1)}, u32[]{:S(2)}, u32[]{:S(2)}) async-start(f32[128,8,128]{2,1,0:T(8,128)} %bitcast.4), calls=%async_computation.2 | async-start | bytes 1048576 | tf_op jit(solution)/shard_map/all_to_all | solution.py:462

commit v3 on v2

--- a/solution.py
+++ b/solution.py
@@ -25,8 +25,6 @@
 PAIRS = FIELDS * GROUP
 MAIN = PAIRS * ROWS
 EDGE = 2 * PAIRS
-EDGE_PAD = 48
-ALL = MAIN + EDGE_PAD
 COLUMNS = ROWS * COLS
 BLOCKS = N_LAT * N_LON
 CIRCLE = COLS * N_LON
@@ -34,25 +32,29 @@
 F32 = jnp.float32
 BF16 = jnp.bfloat16
 VMEM = pl.BlockSpec(memory_space=pltpu.VMEM)
+HBM = pl.BlockSpec(memory_space=pltpu.HBM)
 ANY = pl.BlockSpec(memory_space=pl.ANY)
 SMEM = pl.BlockSpec(memory_space=pltpu.SMEM)
 
 
-def call(kernel, name, out_shapes, scratch, megabytes, *args, scalars=0, stored=(), after=()):
+def call(kernel, name, out_shapes, scratch, megabytes, *args, scalars=0, stored=(), after=(), left=(), taken=()):
     def body(*refs):
         kernel(*refs[: len(args)], *refs[len(args) + len(after) :])
 
     placed = args[:scalars] + tuple(
-        pltpu.with_memory_space_constraint(arg, pltpu.VMEM) for arg in args[scalars:]
+        pltpu.with_memory_space_constraint(arg, pltpu.HBM if index in taken else pltpu.VMEM)
+        for index, arg in enumerate(args[scalars:])
     )
     return pl.pallas_call(
         body,
         out_shape=tuple(
-            jax.ShapeDtypeStruct(shape, kind) if index in stored else pltpu.VMEM(shape, kind)
+            jax.ShapeDtypeStruct(shape, kind) if index in stored + left else pltpu.VMEM(shape, kind)
             for index, (shape, kind) in enumerate(out_shapes)
         ),
-        in_specs=[SMEM] * scalars + [VMEM] * (len(args) - scalars) + [ANY] * len(after),
-        out_specs=(VMEM,) * len(out_shapes),
+        in_specs=[SMEM] * scalars
+        + [HBM if index in taken else VMEM for index in range(len(args) - scalars)]
+        + [ANY] * len(after),
+        out_specs=tuple(ANY if index in left else VMEM for index in range(len(out_shapes))),
         scratch_shapes=scratch,
         compiler_params=pltpu.CompilerParams(vmem_limit_bytes=megabytes << 20),
         name=name,
@@ -82,7 +84,7 @@
 
 def row_tables():
     total = N_LAT * ROWS
-    table = np.zeros((N_LAT, 8, ROWS, COLS), np.float32)
+    table = np.zeros((N_LAT, 9, ROWS, COLS), np.float32)
     rows = np.arange(-1, total + 1)
     latitude = (rows + 0.5) * (math.pi / total) - 0.5 * math.pi
     metric = 1.0 / np.maximum(np.cos(latitude), FLOOR)
@@ -97,7 +99,46 @@
         table[band, 5] = metric[first]
         table[band, 6] = coriolis[first]
         table[band, 7] = float(band > 0)
+        table[band, 8] = float(band % 2 == 0)
     return table
+
+
+def gather_kernel(
+    band_ref, state_ref, rows_ref, filter_ref,
+    out_ref, band_rows_ref, wanted_ref, filter_scratch, done_ref,
+):
+    band = band_ref[0]
+    copies = [
+        pltpu.make_async_copy(
+            state_ref.at[field],
+            out_ref.at[:, field * GROUP * ROWS : (field + 1) * GROUP * ROWS, :],
+            done_ref.at[field],
+        )
+        for field in range(FIELDS)
+    ]
+    copies.append(pltpu.make_async_copy(rows_ref.at[band], band_rows_ref, done_ref.at[FIELDS]))
+    fetch = pltpu.make_async_copy(filter_ref, filter_scratch, done_ref.at[FIELDS + 1])
+    fetch.start()
+    for copy in copies:
+        copy.start()
+    fetch.wait()
+    first = band * ROWS
+    sub = lax.broadcasted_iota(jnp.int32, (ROWS, COLS), 0)
+    wanted = jnp.zeros((ROWS, COLS), jnp.int32)
+    for row in range(ROWS):
+        wanted = jnp.where(sub == row, filter_scratch[first + row], wanted)
+    for pair in range(PAIRS):
+        wanted_ref[pair * ROWS : (pair + 1) * ROWS, :] = wanted
+    beyond = (
+        jnp.minimum(first + ROWS, N_LAT * ROWS - 1), jnp.maximum(first - 1, 0),
+        first + ROWS - 1, first,
+    )
+    for place, row in enumerate(beyond):
+        wanted_ref[MAIN + place * PAIRS : MAIN + (place + 1) * PAIRS, :] = jnp.full(
+            (PAIRS, COLS), filter_scratch[row], jnp.int32
+        )
+    for copy in copies:
+        copy.wait()
 
 
 def pack_kernel(band_ref, state_ref, near_ref, far_ref):
@@ -192,26 +233,59 @@
     lax.fori_loop(0, GROUP, level_step, 0)
 
 
-def inside_kernel(band_ref, state_ref, rows_ref, out_ref):
-    band = band_ref[0]
+def fourier_sums(load, analysis_ref):
+    high, low = zip(*(halves(load(tile)) for tile in range(N_LON)))
+    both = jnp.concatenate(
+        [jnp.concatenate(high, axis=1), jnp.concatenate(low, axis=1)], axis=0
+    )
+    sums = jnp.dot(both, analysis_ref[...], preferred_element_type=F32)
+    rows = sums.shape[0] // 2
+    sums = sums[:rows] + sums[rows:]
+    return sums[:, :COLS] + sums[:, COLS:]
+
+
+def smooth_rows(sums, synthesis_ref):
+    rows = sums.shape[0]
+    high, low = halves(sums)
+    both = jnp.concatenate(
+        [jnp.concatenate([high, high], axis=1), jnp.concatenate([low, low], axis=1)], axis=0
+    )
+    for pair in range(N_LON // 2):
+        smooth = jnp.dot(
+            both,
+            synthesis_ref[:, pair * 2 * COLS : (pair + 1) * 2 * COLS],
+            preferred_element_type=F32,
+        )
+        smooth = smooth[:rows] + smooth[rows:]
+        yield 2 * pair, smooth[:, :COLS]
+        yield 2 * pair + 1, smooth[:, COLS:]
+
+
+def filter_main(stepped_ref, target_ref, wanted_ref, analysis_ref, synthesis_ref):
+    sums = fourier_sums(lambda tile: stepped_ref[tile], analysis_ref)
+    for tile, smooth in smooth_rows(sums, synthesis_ref):
+        target_ref[tile] = jnp.where(wanted_ref[:MAIN, :] == 1, smooth, stepped_ref[tile])
+
+
+def inside_kernel(
+    state_ref, rows_ref, wanted_ref, analysis_ref, synthesis_ref, out_ref, stepped_ref
+):
     step_main(
-        state_ref, out_ref, lambda tile, pair: 0.0, lambda tile, pair: 0.0,
-        rows_ref[band, 0], rows_ref[band, 1],
-    )
+        state_ref, stepped_ref, lambda tile, pair: 0.0, lambda tile, pair: 0.0,
+        rows_ref[0], rows_ref[1],
+    )
+    filter_main(stepped_ref, out_ref, wanted_ref, analysis_ref, synthesis_ref)
 
 
 def dynamics_kernel(
-    band_ref, filter_ref, state_ref, inside_ref, near_ref, far_ref, rows_ref, analysis_ref, synthesis_ref,
-    out_ref, north_ref, south_ref, stepped_ref, current_ref, split_ref,
+    state_ref, inside_ref, near_ref, far_ref, rows_ref, wanted_ref, analysis_ref,
+    synthesis_ref, out_ref, north_ref, south_ref, stepped_ref, current_ref, edge_ref,
 ):
-    band = band_ref[0]
-    first = band * ROWS
-    sub = lax.broadcasted_iota(jnp.int32, (ROWS, COLS), 0)
     lane_edge = lax.broadcasted_iota(jnp.int32, (GROUP, COLS), 1)
-    metric = rows_ref[band, 0]
-    coriolis = rows_ref[band, 1]
-
-    even = lax.broadcasted_iota(jnp.int32, (EDGE, COLS), 0) * 0 + band % 2 == 0
+    metric = rows_ref[0]
+    coriolis = rows_ref[1]
+
+    even = jnp.concatenate([rows_ref[8]] * (EDGE // ROWS), axis=0) > 0.5
     for tile in range(N_LON):
         near_rows = near_ref[tile]
         far_rows = far_ref[tile]
@@ -220,9 +294,9 @@
 
     def step_edge(side):
         base = 2 + 3 * side
-        metric_edge = rows_ref[band, base][:GROUP]
-        coriolis_edge = rows_ref[band, base + 1][:GROUP]
-        exists = rows_ref[band, base + 2][:GROUP]
+        metric_edge = rows_ref[base][:GROUP]
+        coriolis_edge = rows_ref[base + 1][:GROUP]
+        exists = rows_ref[base + 2][:GROUP]
         halo = (north_ref, south_ref)[side]
         near = (0, PAIRS)[side]
         far = (PAIRS, 0)[side]
@@ -250,54 +324,25 @@
                 if extra is not None:
                     result = result + extra
                 place = MAIN + side * PAIRS + field * GROUP
-                stepped_ref[tile, place : place + GROUP, :] = jnp.where(exists > 0.5, result, 0.0)
-                stepped_ref[tile, own_rows, :] = stepped_ref[tile, own_rows, :] + given * here
-
-    wanted = jnp.zeros((ROWS, COLS), jnp.int32)
-    for row in range(ROWS):
-        wanted = jnp.where(sub == row, filter_ref[first + row], wanted)
-    wanted_main = jnp.concatenate([wanted] * PAIRS, axis=0) == 1
-    wanted_above = filter_ref[jnp.minimum(first + ROWS, N_LAT * ROWS - 1)]
-    wanted_below = filter_ref[jnp.maximum(first - 1, 0)]
-    edge_row = lax.broadcasted_iota(jnp.int32, (EDGE_PAD, COLS), 0)
-    wanted_edge = jnp.where(edge_row < PAIRS, wanted_above, wanted_below) == 1
-
-    def polar_filter(rows, target):
-        for tile in range(N_LON):
-            high, low = halves(stepped_ref[tile, :rows, :])
-            split_ref[:rows, tile * COLS : (tile + 1) * COLS] = high
-            split_ref[rows : 2 * rows, tile * COLS : (tile + 1) * COLS] = low
-        sums = jnp.dot(split_ref[: 2 * rows, :], analysis_ref[...], preferred_element_type=F32)
-        sums = sums[:rows] + sums[rows:]
-        sums = sums[:, :COLS] + sums[:, COLS:]
-        high, low = halves(sums)
-        both = jnp.concatenate(
-            [jnp.concatenate([high, high], axis=1), jnp.concatenate([low, low], axis=1)], axis=0
-        )
-        for pair in range(N_LON // 2):
-            smooth = jnp.dot(
-                both,
-                synthesis_ref[:, pair * 2 * COLS : (pair + 1) * 2 * COLS],
-                preferred_element_type=F32,
-            )
-            smooth = smooth[:rows] + smooth[rows:]
-            for side in range(2):
-                tile = 2 * pair + side
-                piece = smooth[:, side * COLS : (side + 1) * COLS]
-                target[tile, :MAIN, :] = jnp.where(
-                    wanted_main, piece[:MAIN], stepped_ref[tile, :MAIN, :]
-                )
-                if rows > MAIN:
-                    target[tile, MAIN:rows, :] = jnp.where(
-                        wanted_edge, piece[MAIN:], stepped_ref[tile, MAIN:rows, :]
-                    )
-
-    stepped_ref[:, MAIN + EDGE :, :] = jnp.zeros((N_LON, ALL - MAIN - EDGE, COLS), F32)
-    for tile in range(N_LON):
-        stepped_ref[tile, :MAIN, :] = inside_ref[tile]
+                result = jnp.where(exists > 0.5, result, 0.0)
+                place = side * PAIRS + field * GROUP
+                edge_ref[tile, place : place + GROUP, :] = result
+                place = EDGE + place
+                edge_ref[tile, place : place + GROUP, :] = given * here
+
     step_edge(0)
     step_edge(1)
-    polar_filter(ALL, current_ref)
+    sums = fourier_sums(lambda tile: edge_ref[tile], analysis_ref)
+    for tile, smooth in smooth_rows(sums, synthesis_ref):
+        edge = jnp.where(wanted_ref[MAIN:, :] == 1, smooth, edge_ref[tile])
+        current_ref[tile, :MAIN, :] = inside_ref[tile]
+        current_ref[tile, MAIN:, :] = edge[:EDGE]
+        for side, own in enumerate((ROWS - 1, 0)):
+            rows = pl.ds(own, PAIRS, stride=ROWS)
+            place = EDGE + side * PAIRS
+            current_ref[tile, rows, :] = (
+                current_ref[tile, rows, :] + edge[place : place + PAIRS]
+            )
     step_main(
         current_ref,
         stepped_ref,
@@ -306,42 +351,47 @@
         metric,
         coriolis,
     )
-    polar_filter(MAIN, out_ref)
+    filter_main(stepped_ref, out_ref, wanted_ref, analysis_ref, synthesis_ref)
 
 
 def prepare_kernel(mixing_ref, map_ref, gain_ref, inverse_ref, order_ref):
     mix = mixing_ref[...]
-
-    def level_step(level, above):
-        inside = jnp.where((level == 0) | (level == LEVELS - 1), 1.0, 2.0)
-        inverse = 1.0 / (1.0 + inside * mix - mix * above)
+    gain = jnp.zeros_like(mix)
+    for level in range(LEVELS):
+        inside = 1.0 if level in (0, LEVELS - 1) else 2.0
+        inverse = 1.0 / (1.0 + inside * mix - mix * gain)
         gain = mix * inverse
         gain_ref[level] = gain
         inverse_ref[level] = inverse
-        return gain
-
-    lax.fori_loop(0, LEVELS, level_step, jnp.zeros_like(mix))
 
     target = map_ref[...] // COLUMNS
     before = lax.broadcasted_iota(jnp.int32, (COLS, 2 * COLS), 0)
     after = lax.broadcasted_iota(jnp.int32, (COLS, 2 * COLS), 1)
     counter = jnp.where((before < after) | (after >= COLS), 1.0, 0.0).astype(BF16)
     block = lax.broadcasted_iota(jnp.int32, (BLOCKS, COLS), 0)
-    place = lax.broadcasted_iota(jnp.int32, (COLUMNS, COLS), 0)
+    sub = lax.broadcasted_iota(jnp.int32, (2 * ROWS, COLS), 0)
     earlier = jnp.zeros((BLOCKS, COLS), F32)
+    one = jnp.ones((2 * ROWS, COLS), BF16)
+    zero = jnp.zeros((2 * ROWS, COLS), BF16)
     for row in range(ROWS):
         goal = target[row : row + 1, :]
         chosen = jnp.where(block == goal, 1.0, 0.0)
         counted = jnp.dot(chosen.astype(BF16), counter, preferred_element_type=F32)
         rank = jnp.sum(chosen * (counted[:, :COLS] + earlier), axis=0, keepdims=True)
         earlier = earlier + counted[:, COLS:]
-        seat = goal * ROWS + rank.astype(jnp.int32)
-        order_ref[:, row * COLS : (row + 1) * COLS] = jnp.where(place == seat, 1.0, 0.0).astype(BF16)
+        seat = rank.astype(jnp.int32)
+        pair = jnp.where(
+            sub == seat, goal, jnp.where(sub == seat + ROWS, goal - 1, -1)
+        ).astype(F32).astype(BF16)
+        for even in range(0, BLOCKS, 2):
+            order_ref[even * ROWS : (even + 2) * ROWS, row * COLS : (row + 1) * COLS] = jnp.where(
+                pair == jnp.asarray(even, BF16), one, zero
+            )
 
 
 def physics_kernel(
     dyn_ref, mixing_ref, sun_ref, map_ref, gain_ref, inverse_ref, order_ref,
-    out_ref, send_ref, heating_ref, table_ref,
+    stored_ref, send_ref, out_ref, heating_ref, table_ref, done_ref,
 ):
     zero = jnp.zeros((ROWS, COLS), F32)
 
@@ -382,6 +432,8 @@
 
     lax.fori_loop(0, N_LON, backward, (zero,) * FIELDS)
 
+    store = pltpu.make_async_copy(out_ref, stored_ref, done_ref)
+    store.start()
     slots = (map_ref[...] % COLUMNS).astype(F32)
     top = lax.broadcasted_iota(jnp.int32, (COLS - LEVELS, COLS), 0) == 0
     for row in range(ROWS):
@@ -394,6 +446,7 @@
         order_ref[...], table_ref[...], (((1,), (1,)), ((), ())), preferred_element_type=F32
     )
     send_ref[...] = sent[:, :COLS] + sent[:, COLS:]
+    store.wait()
 
 
 def place_kernel(got_ref, out_ref):
@@ -413,10 +466,18 @@
     band = lax.axis_index("lat").astype(jnp.int32).reshape(1)
 
     state, band = lax.optimization_barrier((state, band))
-    by_group = state.reshape(FIELDS, N_LON, GROUP, ROWS, COLS).transpose(1, 0, 2, 3, 4)
-    circles = lax.all_to_all(
-        by_group.reshape(N_LON, MAIN, COLS), "lon", split_axis=0, concat_axis=0, tiled=True
-    )
+    by_group, band_rows, wanted = call(
+        gather_kernel, "gather",
+        (
+            ((N_LON, MAIN, COLS), F32),
+            (rows.shape[1:], F32),
+            ((MAIN + 2 * EDGE, COLS), jnp.int32),
+        ),
+        [pltpu.SMEM((N_LAT * ROWS,), jnp.int32), pltpu.SemaphoreType.DMA((FIELDS + 2,))], 1,
+        band, state.reshape(FIELDS, N_LON, GROUP * ROWS, COLS), rows, filter_rows,
+        scalars=1, taken=(0, 1, 2),
+    )
+    circles = lax.all_to_all(by_group, "lon", split_axis=0, concat_axis=0, tiled=True)
     edge = ((N_LON, EDGE, COLS), F32)
     to_near, to_far = call(pack_kernel, "pack", (edge, edge), [], 4, band, circles, scalars=1)
     near = lax.ppermute(to_near, "lat", [(i, i ^ 1) for i in range(N_LAT)])
@@ -424,8 +485,10 @@
         to_far, "lat", [(i, ((i + 1) ^ 1) - 1) for i in range(1, N_LAT - 1)]
     )
     (inside,) = call(
-        inside_kernel, "inside", (((N_LON, MAIN, COLS), F32),), [], 4, band, circles, rows,
-        scalars=1, after=(to_near, to_far),
+        inside_kernel, "inside", (((N_LON, MAIN, COLS), F32),),
+        [pltpu.VMEM((N_LON, MAIN, COLS), F32)], 8,
+        circles, band_rows, wanted, analysis, synthesis,
+        after=(to_near, to_far),
     )
     levels = ((LEVELS, ROWS, COLS), F32)
     gain, inverse, order = call(
@@ -440,13 +503,12 @@
         [
             pltpu.VMEM((N_LON, EDGE, COLS), F32),
             pltpu.VMEM((N_LON, EDGE, COLS), F32),
-            pltpu.VMEM((N_LON, ALL, COLS), F32),
-            pltpu.VMEM((N_LON, ALL, COLS), F32),
-            pltpu.VMEM((2 * ALL, CIRCLE), BF16),
+            pltpu.VMEM((N_LON, MAIN, COLS), F32),
+            pltpu.VMEM((N_LON, MAIN + EDGE, COLS), F32),
+            pltpu.VMEM((N_LON, 2 * EDGE, COLS), F32),
         ],
         16,
-        band, filter_rows, circles, inside, near, far, rows, analysis, synthesis,
-        scalars=2,
+        circles, inside, near, far, band_rows, wanted, analysis, synthesis,
         after=(gain,),
     )
     columns = lax.all_to_all(dyn, "lon", split_axis=0, concat_axis=0, tiled=True)
@@ -454,10 +516,15 @@
         physics_kernel,
         "physics",
         (((FIELDS, LEVELS, ROWS, COLS), F32), ((COLUMNS, COLS), F32)),
-        [pltpu.VMEM((LEVELS * ROWS, COLS), F32), pltpu.VMEM((2 * COLS, COLUMNS), BF16)],
+        [
+            pltpu.VMEM((FIELDS, LEVELS, ROWS, COLS), F32),
+            pltpu.VMEM((LEVELS * ROWS, COLS), F32),
+            pltpu.VMEM((2 * COLS, COLUMNS), BF16),
+            pltpu.SemaphoreType.DMA(()),
+        ],
         12,
         columns, mixing, insolation, block_map, gain, inverse, order,
-        stored=(),
+        left=(0,),
     )
     got = lax.all_to_all(
         sent.reshape(BLOCKS, ROWS, COLS), ("lat", "lon"), split_axis=0, concat_axis=0, tiled=True

time: 92.1 us -> 89.6 us (0.973)
  blocking collectives: 49.5 us -> 70.4 us
  waiting for transfers between devices: 13.2 us -> 0.65 us
  starting transfers between devices: 12.4 us -> 5.05 us
  local copies, waits for them, and re-layouts: 2.54 us -> 0.02 us
    all_to_all x1 -> x2, blocking collectives: 27.2 us -> 47.9 us  [the longest x1 27.3 us: per_device(): lax.all_to_all(by_group, 'lon', split_axis=0, concat_axis=0, tiled=True)]
    all_to_all x1 -> x0, waiting for transfers between devices: 12.4 us -> none  [per_device(): lax.all_to_all(sent.reshape(BLOCKS, ROWS, COLS), ('lat', 'lon'), split_ax...]
    all_to_all x1 -> x0, starting transfers between devices: 7.49 us -> none  [per_device(): lax.all_to_all(sent.reshape(BLOCKS, ROWS, COLS), ('lat', 'lon'), split_ax...]
    reshape x1 -> x0, local copies, waits for them, and re-layouts: 1.44 us -> none  [per_device(): state.reshape(FIELDS, N_LON, GROUP, ROWS, COLS).transpose(1, 0, 2, 3, 4)]
    unnamed x15 -> x10, local copies, waits for them, and re-layouts: 1.1 us -> 0.02 us
    pallas_call x6 -> x7, Pallas kernels: 13.4 us -> 12.5 us  [call(): pl.pallas_call(body, out_shape=tuple((jax.ShapeDtypeStruct(shape, kind) i...]
  transfers between devices with their start and end apart: 3 -> 2, of which waited for: 2 -> 1; matrix products, arithmetic and copies ran while one was open for 1% -> 0% of each run, Pallas kernels for 4% -> 4%
where the time goes in v3:
time: 89.6 us; the launch traced here: 89.4 us
  blocking collectives  70.4 us (79%)
  Pallas kernels  12.5 us (14%)
  starting transfers between devices  5.05 us (6%)
    all_to_all x1, blocking collectives, per_device(): lax.all_to_all(by_group, 'lon', split_axis=0, concat_axis=0, tiled=True)  27.3 us
    all_to_all x1, blocking collectives, per_device(): lax.all_to_all(dyn, 'lon', split_axis=0, concat_axis=0, tiled=True)  22.5 us
    all_to_all x1, blocking collectives, per_device(): lax.all_to_all(sent.reshape(BLOCKS, ROWS, COLS), ('lat', 'lon'), split_ax...  20.6 us
    pallas_call x7, Pallas kernels, call(): pl.pallas_call(body, out_shape=tuple((jax.ShapeDtypeStruct(shape, kind) i...  12.5 us
    ppermute x1, starting transfers between devices, per_device(): lax.ppermute(to_far, 'lat', [(i, (i + 1 ^ 1) - 1) for i in range(1, N_LAT...  4.96 us
  transfers between devices with their start and end apart: 2, of which 1 were waited for; matrix products, arithmetic and copies ran while one was open for 0% of the time, Pallas kernels for 4%

profile of v3, /device:TPU:1, one launch (start us, length us, event | category | flops | bytes accessed | tf_op | source)
XLA Modules:
  0.0 89.4 jit_solution(14950205217869357001)
XLA Ops:
  0.6 1.3 %gather.1 = (f32[16,160,128]{2,1,0:T(8,128)S(1)}, f32[9,8,128]{2,1,0:T(8,128)S(1)}, s32[240,128]{1,0:T(8,128)S(1)}) custom-call(s32[1]{0:T(128)} %bitcast.refs_0_, f32[4,16,40,128]{3,2,1,0:T(8,128)} %bitcast.6, f32[8,9,8,128]{3,2,1,0:T(8,128)} %constant.14.clone.refs_2_, s32[64]{0:T(128)} %refs_3_.3), custom_call_target="tpu_custom_call" | custom-call | tf_op jit(solution)/shard_map/gather/pallas_call | solution.py:48
  2.0 0.0 copy-start.1
  2.0 27.3 %all_to_all.15.refs_1_.refs_0_ = f32[16,160,128]{2,1,0:T(8,128)S(1)} all-to-all(f32[16,160,128]{2,1,0:T(8,128)S(1)} %get-tuple-element.16), channel_id=1, replica_groups=mesh['lat'=8,'lon'=16] {'lon'}, dimensions={0} | all-to-all | bytes 2621440 | tf_op jit(solution)/shard_map/all_to_all | solution.py:480
  29.3 0.0 copy-start.2
  29.3 0.0 copy-start.3
  29.3 0.0 copy-start
  29.3 0.1 pack.1
  29.4 5.0 %collective-permute-start.1 = (f32[16,40,128]{2,1,0:T(8,128)S(1)}, f32[16,40,128]{2,1,0:T(8,128)S(1)}, u32[]{:S(2)}, u32[]{:S(2)}) collective-permute-start(f32[16,40,128]{2,1,0:T(8,128)S(1)} %get-tuple-element.20.refs_6_), channel_id=1, source_target_pairs={{16,32},{32,16},{48,64},{64,48},{80,96},{96,80},{17,33},{33,17},{4... | collective-permute-start | bytes 983048 | tf_op jit(solution)/shard_map/ppermute | solution.py:484
  34.4 0.1 collective-permute-start
  34.5 0.0 copy-done.2
  34.5 0.0 copy-done.3
  34.5 1.2 %prepare.1 = (f32[80,8,128]{2,1,0:T(8,128)S(1)}, f32[80,8,128]{2,1,0:T(8,128)S(1)}, bf16[1024,1024]{1,0:T(8,128)(2,1)S(1)}) custom-call(f32[8,128]{1,0:T(8,128)S(1)} %copy-done.2, s32[8,128]{1,0:T(8,128)S(1)} %copy-done.3, f32[16,40,128]{2,1,0:T(8,128)S(1)} %get-tuple-element.19.refs_5_.refs_2_), custom_call_target="tpu_custom_call" | custom-call | tf_op jit(solution)/shard_map/prepare/pallas_call | solution.py:48
  35.7 0.0 copy-done.1
  35.7 0.0 copy-done
  35.7 2.7 %inside.1.refs_1_ = f32[16,160,128]{2,1,0:T(8,128)S(1)} custom-call(f32[16,160,128]{2,1,0:T(8,128)S(1)} %all_to_all.15.refs_1_.refs_0_, f32[9,8,128]{2,1,0:T(8,128)S(1)} %get-tuple-element.17.refs_1_.refs_4_, s32[240,128]{1,0:T(8,128)S(1)} %get-tuple-element.18.refs_2_.refs_5_, bf16[2048,256]{1,0:T(8,128)(2,1)S(1)} %copy-done.1, ...), custom_call_target="tpu_custom_call" | custom-call | tf_op jit(solution)/shard_map/inside/pallas_call | solution.py:48
  38.5 0.7 collective-permute-done.1.refs_3_
  39.1 0.0 collective-permute-done.refs_2_
  39.1 4.1 %dynamics.1 = f32[16,160,128]{2,1,0:T(8,128)S(1)} custom-call(f32[16,160,128]{2,1,0:T(8,128)S(1)} %all_to_all.15.refs_1_.refs_0_, f32[16,160,128]{2,1,0:T(8,128)S(1)} %inside.1.refs_1_, f32[16,40,128]{2,1,0:T(8,128)S(1)} %collective-permute-done.refs_2_, f32[16,40,128]{2,1,0:T(8,128)S(1)} %collective-permute-done.1.refs_3_, ...), custom_call_target="tpu_custom_call" | custom-call | tf_op jit(solution)/shard_map/dynamics/pallas_call | solution.py:48
  43.2 0.0 copy-start.4
  43.2 22.5 %all_to_all.16.refs_0_ = f32[16,160,128]{2,1,0:T(8,128)S(1)} all-to-all(f32[16,160,128]{2,1,0:T(8,128)S(1)} %dynamics.1), channel_id=1, replica_groups=mesh['lat'=8,'lon'=16] {'lon'}, dimensions={0} | all-to-all | bytes 2621440 | tf_op jit(solution)/shard_map/all_to_all | solution.py:514
  65.7 0.0 copy-done.4
  65.7 1.6 %physics.1 = (f32[4,80,8,128]{3,2,1,0:T(8,128)}, f32[1024,128]{1,0:T(8,128)S(1)}) custom-call(f32[16,160,128]{2,1,0:T(8,128)S(1)} %all_to_all.16.refs_0_, f32[8,128]{1,0:T(8,128)S(1)} %copy-done.2, f32[8,128]{1,0:T(8,128)S(1)} %copy-done.4, s32[8,128]{1,0:T(8,128)S(1)} %copy-done.3, f32[80,8,128]{2,1,0:T(8,128)S(1)} %get-tuple-element.21.refs_8_.refs_4_, ...), custom_call_target="tpu_custom_call" | custom-call | tf_op jit(solution)/shard_map/physics/pallas_call | solution.py:48
  67.3 20.6 %all_to_all.17 = f32[128,8,128]{2,1,0:T(8,128)S(1)} all-to-all(f32[128,8,128]{2,1,0:T(8,128)S(1)} %bitcast.5), channel_id=1, replica_groups=mesh['lat'=8,'lon'=16] {'lat','lon'}, dimensions={0} | all-to-all | bytes 1048576 | tf_op jit(solution)/shard_map/all_to_all | solution.py:529
  87.9 1.4 %place.1 = f32[1,80,1024]{2,1,0:T(8,128)} custom-call(f32[1024,128]{1,0:T(8,128)S(1)} %bitcast.4), custom_call_target="tpu_custom_call" | custom-call | tf_op jit(solution)/shard_map/place/pallas_call | solution.py:48
Async XLA Ops:
  2.0 33.8 %copy-start.1 = (bf16[2048,256]{1,0:T(8,128)(2,1)S(1)}, bf16[2048,256]{1,0:T(8,128)(2,1)}, u32[]{:S(2)}) copy-start(bf16[2048,256]{1,0:T(8,128)(2,1)} %constant.12.clone.refs_3_.refs_6_) | copy-start | bytes 3145732
  29.3 5.2 %copy-start.2 = (f32[8,128]{1,0:T(8,128)S(1)}, f32[8,128]{1,0:T(8,128)}, u32[]{:S(2)}) copy-start(f32[8,128]{1,0:T(8,128)} %refs_1_.3) | copy-start | bytes 12292
  29.3 5.2 %copy-start.3 = (s32[8,128]{1,0:T(8,128)S(1)}, s32[8,128]{1,0:T(8,128)}, u32[]{:S(2)}) copy-start(s32[8,128]{1,0:T(8,128)} %refs_3_.4) | copy-start | bytes 12292
  29.3 6.4 %copy-start = (bf16[256,2048]{1,0:T(8,128)(2,1)S(1)}, bf16[256,2048]{1,0:T(8,128)(2,1)}, u32[]{:S(2)}) copy-start(bf16[256,2048]{1,0:T(8,128)(2,1)} %constant.13.clone.refs_4_.refs_7_) | copy-start | bytes 3145732
  29.4 9.7 %collective-permute-start.1 = (f32[16,40,128]{2,1,0:T(8,128)S(1)}, f32[16,40,128]{2,1,0:T(8,128)S(1)}, u32[]{:S(2)}, u32[]{:S(2)}) collective-permute-start(f32[16,40,128]{2,1,0:T(8,128)S(1)} %get-tuple-element.20.refs_6_), channel_id=1, source_target_pairs={{16,32},{32,16},{48,64},{64,48},{80,96},{96,80},{17,33},{33,17},{4... | collective-permute-start | bytes 983048 | tf_op jit(solution)/shard_map/ppermute | solution.py:484
  34.4 4.7 %collective-permute-start = (f32[16,40,128]{2,1,0:T(8,128)S(1)}, f32[16,40,128]{2,1,0:T(8,128)S(1)}, u32[]{:S(2)}, u32[]{:S(2)}) collective-permute-start(f32[16,40,128]{2,1,0:T(8,128)S(1)} %get-tuple-element.19.refs_5_.refs_2_), channel_id=1, source_target_pairs={{0,16},{16,0},{32,48},{48,32},{64,80},{80,64},{96,112},{112,96},{1... | collective-permute-start | bytes 983048 | tf_op jit(solution)/shard_map/ppermute | solution.py:483
  43.2 22.5 %copy-start.4 = (f32[8,128]{1,0:T(8,128)S(1)}, f32[8,128]{1,0:T(8,128)}, u32[]{:S(2)}) copy-start(f32[8,128]{1,0:T(8,128)} %refs_2_.2) | copy-start | bytes 12292

commit v4 on v3

--- a/solution.py
+++ b/solution.py
@@ -244,42 +244,50 @@
     return sums[:, :COLS] + sums[:, COLS:]
 
 
-def smooth_rows(sums, synthesis_ref):
+def smooth_rows(band, sums, both_ref, synthesis_ref, emit):
     rows = sums.shape[0]
     high, low = halves(sums)
-    both = jnp.concatenate(
+    both_ref[...] = jnp.concatenate(
         [jnp.concatenate([high, high], axis=1), jnp.concatenate([low, low], axis=1)], axis=0
     )
-    for pair in range(N_LON // 2):
-        smooth = jnp.dot(
-            both,
-            synthesis_ref[:, pair * 2 * COLS : (pair + 1) * 2 * COLS],
-            preferred_element_type=F32,
-        )
-        smooth = smooth[:rows] + smooth[rows:]
-        yield 2 * pair, smooth[:, :COLS]
-        yield 2 * pair + 1, smooth[:, COLS:]
-
-
-def filter_main(stepped_ref, target_ref, wanted_ref, analysis_ref, synthesis_ref):
+
+    @pl.when(band >= 0)
+    def inverse():
+        for pair in range(N_LON // 2):
+            smooth = jnp.dot(
+                both_ref[...],
+                synthesis_ref[:, pair * 2 * COLS : (pair + 1) * 2 * COLS],
+                preferred_element_type=F32,
+            )
+            smooth = smooth[:rows] + smooth[rows:]
+            emit(2 * pair, smooth[:, :COLS])
+            emit(2 * pair + 1, smooth[:, COLS:])
+
+
+def filter_main(band, stepped_ref, target_ref, wanted_ref, analysis_ref, synthesis_ref, both_ref):
     sums = fourier_sums(lambda tile: stepped_ref[tile], analysis_ref)
-    for tile, smooth in smooth_rows(sums, synthesis_ref):
+
+    def emit(tile, smooth):
         target_ref[tile] = jnp.where(wanted_ref[:MAIN, :] == 1, smooth, stepped_ref[tile])
 
+    smooth_rows(band, sums, both_ref, synthesis_ref, emit)
+
 
 def inside_kernel(
-    state_ref, rows_ref, wanted_ref, analysis_ref, synthesis_ref, out_ref, stepped_ref
+    band_ref, state_ref, rows_ref, wanted_ref, analysis_ref, synthesis_ref,
+    out_ref, stepped_ref, both_ref,
 ):
     step_main(
         state_ref, stepped_ref, lambda tile, pair: 0.0, lambda tile, pair: 0.0,
         rows_ref[0], rows_ref[1],
     )
-    filter_main(stepped_ref, out_ref, wanted_ref, analysis_ref, synthesis_ref)
+    filter_main(band_ref[0], stepped_ref, out_ref, wanted_ref, analysis_ref, synthesis_ref, both_ref)
 
 
 def dynamics_kernel(
-    state_ref, inside_ref, near_ref, far_ref, rows_ref, wanted_ref, analysis_ref,
+    band_ref, state_ref, inside_ref, near_ref, far_ref, rows_ref, wanted_ref, analysis_ref,
     synthesis_ref, out_ref, north_ref, south_ref, stepped_ref, current_ref, edge_ref,
+    both_edge_ref, both_ref,
 ):
     lane_edge = lax.broadcasted_iota(jnp.int32, (GROUP, COLS), 1)
     metric = rows_ref[0]
@@ -333,16 +341,17 @@
     step_edge(0)
     step_edge(1)
     sums = fourier_sums(lambda tile: edge_ref[tile], analysis_ref)
-    for tile, smooth in smooth_rows(sums, synthesis_ref):
+
+    def emit(tile, smooth):
         edge = jnp.where(wanted_ref[MAIN:, :] == 1, smooth, edge_ref[tile])
         current_ref[tile, :MAIN, :] = inside_ref[tile]
         current_ref[tile, MAIN:, :] = edge[:EDGE]
         for side, own in enumerate((ROWS - 1, 0)):
             rows = pl.ds(own, PAIRS, stride=ROWS)
             place = EDGE + side * PAIRS
-            current_ref[tile, rows, :] = (
-                current_ref[tile, rows, :] + edge[place : place + PAIRS]
-            )
+            current_ref[tile, rows, :] = current_ref[tile, rows, :] + edge[place : place + PAIRS]
+
+    smooth_rows(band_ref[0], sums, both_edge_ref, synthesis_ref, emit)
     step_main(
         current_ref,
         stepped_ref,
@@ -351,7 +360,7 @@
         metric,
         coriolis,
     )
-    filter_main(stepped_ref, out_ref, wanted_ref, analysis_ref, synthesis_ref)
+    filter_main(band_ref[0], stepped_ref, out_ref, wanted_ref, analysis_ref, synthesis_ref, both_ref)
 
 
 def prepare_kernel(mixing_ref, map_ref, gain_ref, inverse_ref, order_ref):
@@ -486,9 +495,9 @@
     )
     (inside,) = call(
         inside_kernel, "inside", (((N_LON, MAIN, COLS), F32),),
-        [pltpu.VMEM((N_LON, MAIN, COLS), F32)], 8,
-        circles, band_rows, wanted, analysis, synthesis,
-        after=(to_near, to_far),
+        [pltpu.VMEM((N_LON, MAIN, COLS), F32), pltpu.VMEM((2 * MAIN, 2 * COLS), BF16)], 8,
+        band, circles, band_rows, wanted, analysis, synthesis,
+        scalars=1, after=(to_near, to_far),
     )
     levels = ((LEVELS, ROWS, COLS), F32)
     gain, inverse, order = call(
@@ -506,9 +515,12 @@
             pltpu.VMEM((N_LON, MAIN, COLS), F32),
             pltpu.VMEM((N_LON, MAIN + EDGE, COLS), F32),
             pltpu.VMEM((N_LON, 2 * EDGE, COLS), F32),
+            pltpu.VMEM((4 * EDGE, 2 * COLS), BF16),
+            pltpu.VMEM((2 * MAIN, 2 * COLS), BF16),
         ],
         16,
-        circles, inside, near, far, band_rows, wanted, analysis, synthesis,
+        band, circles, inside, near, far, band_rows, wanted, analysis, synthesis,
+        scalars=1,
         after=(gain,),
     )
     columns = lax.all_to_all(dyn, "lon", split_axis=0, concat_axis=0, tiled=True)

time: 89.6 us -> 88.9 us (level)
  Pallas kernels: 12.5 us -> 11.2 us
    pallas_call x7, Pallas kernels: 12.5 us -> 11.2 us  [call(): pl.pallas_call(body, out_shape=tuple((jax.ShapeDtypeStruct(shape, kind) i...]
where the time goes in v4:
time: 88.9 us; the launch traced here: 88.6 us
  blocking collectives  70.4 us (79%)
  Pallas kernels  11.2 us (13%)
  starting transfers between devices  5.05 us (6%)
  waiting for transfers between devices  1.23 us (1%)
    all_to_all x1, blocking collectives, per_device(): lax.all_to_all(by_group, 'lon', split_axis=0, concat_axis=0, tiled=True)  27.3 us
    all_to_all x1, blocking collectives, per_device(): lax.all_to_all(dyn, 'lon', split_axis=0, concat_axis=0, tiled=True)  23.3 us
    all_to_all x1, blocking collectives, per_device(): lax.all_to_all(sent.reshape(BLOCKS, ROWS, COLS), ('lat', 'lon'), split_ax...  19.8 us
    pallas_call x7, Pallas kernels, call(): pl.pallas_call(body, out_shape=tuple((jax.ShapeDtypeStruct(shape, kind) i...  11.2 us
    ppermute x1, starting transfers between devices, per_device(): lax.ppermute(to_far, 'lat', [(i, (i + 1 ^ 1) - 1) for i in range(1, N_LAT...  4.96 us
  transfers between devices with their start and end apart: 2, of which 1 were waited for; matrix products, arithmetic and copies ran while one was open for 0% of the time, Pallas kernels for 4%

profile of v4, /device:TPU:1, one launch (start us, length us, event | category | flops | bytes accessed | tf_op | source)
XLA Modules:
  0.0 88.6 jit_solution(10979748701343548671)
XLA Ops:
  0.6 1.3 %gather.1 = (f32[16,160,128]{2,1,0:T(8,128)S(1)}, f32[9,8,128]{2,1,0:T(8,128)S(1)}, s32[240,128]{1,0:T(8,128)S(1)}) custom-call(s32[1]{0:T(128)} %bitcast.refs_0_, f32[4,16,40,128]{3,2,1,0:T(8,128)} %bitcast.6, f32[8,9,8,128]{3,2,1,0:T(8,128)} %constant.14.clone.refs_2_, s32[64]{0:T(128)} %refs_3_.2), custom_call_target="tpu_custom_call" | custom-call | tf_op jit(solution)/shard_map/gather/pallas_call | solution.py:48
  2.0 0.0 copy-start.1
  2.0 27.3 %all_to_all.15.refs_1_ = f32[16,160,128]{2,1,0:T(8,128)S(1)} all-to-all(f32[16,160,128]{2,1,0:T(8,128)S(1)} %get-tuple-element.16), channel_id=1, replica_groups=mesh['lat'=8,'lon'=16] {'lon'}, dimensions={0} | all-to-all | bytes 2621440 | tf_op jit(solution)/shard_map/all_to_all | solution.py:489
  29.3 0.0 copy-start.2
  29.3 0.0 copy-start.3
  29.3 0.0 copy-start
  29.3 0.1 pack.1
  29.4 5.0 %collective-permute-start.1 = (f32[16,40,128]{2,1,0:T(8,128)S(1)}, f32[16,40,128]{2,1,0:T(8,128)S(1)}, u32[]{:S(2)}, u32[]{:S(2)}) collective-permute-start(f32[16,40,128]{2,1,0:T(8,128)S(1)} %get-tuple-element.20.refs_7_), channel_id=1, source_target_pairs={{16,32},{32,16},{48,64},{64,48},{80,96},{96,80},{17,33},{33,17},{4... | collective-permute-start | bytes 983048 | tf_op jit(solution)/shard_map/ppermute | solution.py:493
  34.4 0.1 collective-permute-start
  34.5 0.0 copy-done.2
  34.5 0.0 copy-done.3
  34.5 1.2 %prepare.1 = (f32[80,8,128]{2,1,0:T(8,128)S(1)}, f32[80,8,128]{2,1,0:T(8,128)S(1)}, bf16[1024,1024]{1,0:T(8,128)(2,1)S(1)}) custom-call(f32[8,128]{1,0:T(8,128)S(1)} %copy-done.2, s32[8,128]{1,0:T(8,128)S(1)} %copy-done.3, f32[16,40,128]{2,1,0:T(8,128)S(1)} %get-tuple-element.19.refs_6_.refs_2_), custom_call_target="tpu_custom_call" | custom-call | tf_op jit(solution)/shard_map/prepare/pallas_call | solution.py:48
  35.7 0.0 copy-done.1
  35.7 0.0 copy-done
  35.8 2.1 %inside.1.refs_2_ = f32[16,160,128]{2,1,0:T(8,128)S(1)} custom-call(s32[1]{0:T(128)} %bitcast.refs_0_, f32[16,160,128]{2,1,0:T(8,128)S(1)} %all_to_all.15.refs_1_, f32[9,8,128]{2,1,0:T(8,128)S(1)} %get-tuple-element.17.refs_2_.refs_5_, s32[240,128]{1,0:T(8,128)S(1)} %get-tuple-element.18.refs_3_.refs_6_, bf16[2048,256]{1,0:T(8,128)(2,1)S(1)} %copy-done.1, ...), custom_call_target="tpu_custom_call" | custom-call | tf_op jit(solution)/shard_map/inside/pallas_call | solution.py:48
  37.9 1.2 %collective-permute-done.1.refs_4_ = f32[16,40,128]{2,1,0:T(8,128)S(1)} collective-permute-done((f32[16,40,128]{2,1,0:T(8,128)S(1)}, f32[16,40,128]{2,1,0:T(8,128)S(1)}, u32[]{:S(2)}, u32[]{:S(2)}) %collective-permute-start.1) | collective-permute-done | bytes 327712 | tf_op jit(solution)/shard_map/ppermute | solution.py:493
  39.1 0.0 collective-permute-done.refs_3_
  39.1 3.3 %dynamics.1 = f32[16,160,128]{2,1,0:T(8,128)S(1)} custom-call(s32[1]{0:T(128)} %bitcast.refs_0_, f32[16,160,128]{2,1,0:T(8,128)S(1)} %all_to_all.15.refs_1_, f32[16,160,128]{2,1,0:T(8,128)S(1)} %inside.1.refs_2_, f32[16,40,128]{2,1,0:T(8,128)S(1)} %collective-permute-done.refs_3_, f32[16,40,128]{2,1,0:T(8,128)S(1)} %collective-permute-done.1.refs_4_, ...), custom_call_target="tpu_custom_call" | custom-call | tf_op jit(solution)/shard_map/dynamics/pallas_call | solution.py:48
  42.5 0.0 copy-start.4
  42.5 23.3 %all_to_all.16.refs_0_ = f32[16,160,128]{2,1,0:T(8,128)S(1)} all-to-all(f32[16,160,128]{2,1,0:T(8,128)S(1)} %dynamics.1), channel_id=1, replica_groups=mesh['lat'=8,'lon'=16] {'lon'}, dimensions={0} | all-to-all | bytes 2621440 | tf_op jit(solution)/shard_map/all_to_all | solution.py:526
  65.8 0.0 copy-done.4
  65.8 1.6 %physics.1 = (f32[4,80,8,128]{3,2,1,0:T(8,128)}, f32[1024,128]{1,0:T(8,128)S(1)}) custom-call(f32[16,160,128]{2,1,0:T(8,128)S(1)} %all_to_all.16.refs_0_, f32[8,128]{1,0:T(8,128)S(1)} %copy-done.2, f32[8,128]{1,0:T(8,128)S(1)} %copy-done.4, s32[8,128]{1,0:T(8,128)S(1)} %copy-done.3, f32[80,8,128]{2,1,0:T(8,128)S(1)} %get-tuple-element.21.refs_9_.refs_4_, ...), custom_call_target="tpu_custom_call" | custom-call | tf_op jit(solution)/shard_map/physics/pallas_call | solution.py:48
  67.4 19.8 %all_to_all.17 = f32[128,8,128]{2,1,0:T(8,128)S(1)} all-to-all(f32[128,8,128]{2,1,0:T(8,128)S(1)} %bitcast.5), channel_id=1, replica_groups=mesh['lat'=8,'lon'=16] {'lat','lon'}, dimensions={0} | all-to-all | bytes 1048576 | tf_op jit(solution)/shard_map/all_to_all | solution.py:541
  87.2 1.4 %place.1 = f32[1,80,1024]{2,1,0:T(8,128)} custom-call(f32[1024,128]{1,0:T(8,128)S(1)} %bitcast.4), custom_call_target="tpu_custom_call" | custom-call | tf_op jit(solution)/shard_map/place/pallas_call | solution.py:48
Async XLA Ops:
  2.0 33.8 %copy-start.1 = (bf16[2048,256]{1,0:T(8,128)(2,1)S(1)}, bf16[2048,256]{1,0:T(8,128)(2,1)}, u32[]{:S(2)}) copy-start(bf16[2048,256]{1,0:T(8,128)(2,1)} %constant.12.clone.refs_4_.refs_7_) | copy-start | bytes 3145732
  29.3 5.2 %copy-start.2 = (f32[8,128]{1,0:T(8,128)S(1)}, f32[8,128]{1,0:T(8,128)}, u32[]{:S(2)}) copy-start(f32[8,128]{1,0:T(8,128)} %refs_1_.3) | copy-start | bytes 12292
  29.3 5.2 %copy-start.3 = (s32[8,128]{1,0:T(8,128)S(1)}, s32[8,128]{1,0:T(8,128)}, u32[]{:S(2)}) copy-start(s32[8,128]{1,0:T(8,128)} %refs_3_.3) | copy-start | bytes 12292
  29.3 6.5 %copy-start = (bf16[256,2048]{1,0:T(8,128)(2,1)S(1)}, bf16[256,2048]{1,0:T(8,128)(2,1)}, u32[]{:S(2)}) copy-start(bf16[256,2048]{1,0:T(8,128)(2,1)} %constant.13.clone.refs_5_.refs_8_) | copy-start | bytes 3145732
  29.4 9.7 %collective-permute-start.1 = (f32[16,40,128]{2,1,0:T(8,128)S(1)}, f32[16,40,128]{2,1,0:T(8,128)S(1)}, u32[]{:S(2)}, u32[]{:S(2)}) collective-permute-start(f32[16,40,128]{2,1,0:T(8,128)S(1)} %get-tuple-element.20.refs_7_), channel_id=1, source_target_pairs={{16,32},{32,16},{48,64},{64,48},{80,96},{96,80},{17,33},{33,17},{4... | collective-permute-start | bytes 983048 | tf_op jit(solution)/shard_map/ppermute | solution.py:493
  34.4 4.7 %collective-permute-start = (f32[16,40,128]{2,1,0:T(8,128)S(1)}, f32[16,40,128]{2,1,0:T(8,128)S(1)}, u32[]{:S(2)}, u32[]{:S(2)}) collective-permute-start(f32[16,40,128]{2,1,0:T(8,128)S(1)} %get-tuple-element.19.refs_6_.refs_2_), channel_id=1, source_target_pairs={{0,16},{16,0},{32,48},{48,32},{64,80},{80,64},{96,112},{112,96},{1... | collective-permute-start | bytes 983048 | tf_op jit(solution)/shard_map/ppermute | solution.py:492
  42.5 23.3 %copy-start.4 = (f32[8,128]{1,0:T(8,128)S(1)}, f32[8,128]{1,0:T(8,128)}, u32[]{:S(2)}) copy-start(f32[8,128]{1,0:T(8,128)} %refs_2_.2) | copy-start | bytes 12292
